TPU v7x, 32 devices: a whole 2x2x4 slice. The times are simulated.
32 devices in a mesh: rows: 8 (over y, x, core), cols: 4 (over z).
Axes of the slice: x: 2, y: 2, z: 4, core: 2. Of those that a mesh axis runs over, the one named last changes fastest.
Arguments:
- gradient: bfloat16 [32, 16384], P('rows', 'cols'), may hold values from -6 to 6
- basis: float32 [16384, 16384], P('cols', 'rows'), may hold values from -0.046875 to 0.046875
- moment: float32 [32, 16384], P('cols', 'rows'), may hold values from -2 to 2
- second: float32 [32, 16384], P('cols', 'rows'), may hold values from 0.05 to 2
Outputs:
- update: float32 [32, 16384], P('rows', 'cols')
- moment_new: float32 [32, 16384], P('cols', 'rows')
- second_new: float32 [32, 16384], P('cols', 'rows')
All inputs are finite; a program needn't handle non-finite values.
Results may differ from a plain program's by a relative error of at most 0.0003.
Values may be sent and summed in bfloat16 or wider, within the bound.
No kernel may reach another device: no remote copies, remote signals or barrier semaphores. Data moves between devices by JAX's collectives and lax.ppermute only.
A program may use at most 64 MiB of HBM per device.

v0:
```python
import jax
import jax.numpy as jnp
from jax import lax
from jax.sharding import PartitionSpec as P


def adam_moments(moment, second, rotated):
    moment_new = 0.9 * moment + 0.1 * rotated
    second_new = 0.95 * second + 0.05 * rotated * rotated
    normed = moment_new / (1.0 - 0.9**10) / (jnp.sqrt(second_new / (1.0 - 0.95**10)) + 1e-08)
    return (moment_new, second_new, normed)


def body(gradient, basis, moment, second):
    gathered = lax.all_gather(gradient, "rows", axis=0, tiled=True)
    partial_value = jnp.dot(
        gathered.astype(jnp.float32),
        basis,
        precision=lax.Precision.HIGHEST,
        preferred_element_type=jnp.float32,
    )
    rotated = lax.psum_scatter(partial_value, "cols", scatter_dimension=0, tiled=True)
    moment_new, second_new, normed = adam_moments(moment, second, rotated)
    normed_all = lax.all_gather(normed, "cols", axis=0, tiled=True)
    update = lax.psum_scatter(
        lax.dot_general(
            normed_all,
            basis,
            (((1,), (1,)), ((), ())),
            precision=lax.Precision.HIGHEST,
            preferred_element_type=jnp.float32,
        ),
        "rows",
        scatter_dimension=0,
        tiled=True,
    )
    return (update, moment_new, second_new)


def solution(mesh):
    placed = (P("rows", "cols"), P("cols", "rows"), P("cols", "rows"), P("cols", "rows"))
    return jax.shard_map(
        body,
        mesh=mesh,
        in_specs=placed,
        out_specs=(P("rows", "cols"), P("cols", "rows"), P("cols", "rows")),
        check_vma=False,
    )
```

profile of v0, /device:TPU:0, one launch (start us, length us, event | category | flops | bytes accessed | tf_op | source)
XLA Modules:
  0.0 167.4 jit_solution(7342445904849064502)
XLA Ops:
  7.2 0.0 copy-start
  7.2 0.0 copy-start.1
  7.2 0.0 reduce-scatter.2.cloned.1.call-start
  7.2 11.0 %all-gather = bf16[8,4,4096]{2,1,0:T(4,128)(2,1)S(1)} all-gather(bf16[1,4,4096]{2,1,0:T(4,128)(2,1)} %bitcast.6), channel_id=1, replica_groups=mesh['rows'=8,'cols'=4] {'rows'}, dimensions={0}, use_global_device_ids=true | all-gather | bytes 294912 | tf_op jit(solution)/shard_map/all_gather | solution.py:15
  18.2 0.1 reshape.7
  18.3 0.0 copy-start.2
  18.3 16.9 %fusion.2 = f32[32,2048]{1,0:T(8,128)} fusion(bf16[32,4096]{1,0:T(8,128)(2,1)S(1)} %reshape.7, f32[4096,2048]{1,0:T(8,128)} %param.5), kind=kOutput, calls=%fused_computation.5 | convolution fusion | flops 3221225472 | bytes 34078720 | tf_op jit(solution)/shard_map/dot_general | solution.py:16
  35.2 0.0 reduce-scatter.2.cloned.1.call-update
  35.3 0.0 all-reduce.3.cloned.1.call-start
  35.3 20.4 %reduce-scatter.2.cloned.1.call-done = f32[8,2048]{1,0:T(8,128)} async-done(((f32[32,2048]{1,0:T(8,128)}), f32[8,2048]{1,0:T(8,128)}) %reduce-scatter.2.cloned.1.call-update) | async-done | bytes 65552 | tf_op jit(solution)/shard_map/reduce_scatter | solution.py:22
  55.7 0.0 copy-done
  55.7 0.0 copy-done.1
  55.7 1.5 add_divide_fusion
  57.2 13.9 %all_gather.7 = f32[32,2048]{1,0:T(8,128)S(1)} all-gather(f32[8,2048]{1,0:T(8,128)S(1)} %get-tuple-element.3), channel_id=1, replica_groups=mesh['rows'=8,'cols'=4] {'cols'}, dimensions={0}, use_global_device_ids=true | all-gather | bytes 327680 | tf_op jit(solution)/shard_map/all_gather | solution.py:24
  71.1 34.3 %fusion.3 = f32[32,4096]{1,0:T(8,128)} fusion(f32[32,2048]{1,0:T(8,128)S(1)} %all_gather.7, f32[4096,2048]{1,0:T(8,128)} %param.5), kind=kOutput, calls=%fused_computation.6 | convolution fusion | flops 3221225472 | bytes 34340864 | tf_op jit(solution)/shard_map/dot_general | solution.py:26
  105.4 0.0 all-reduce.3.cloned.1.call-update
  105.5 0.0 copy-done.2
  105.5 0.6 dynamic-slice
  106.7 52.3 %all-reduce.3.cloned.1.call-done = f32[32,4096]{1,0:T(8,128)} async-done(((f32[32,4096]{1,0:T(8,128)}), f32[32,4096]{1,0:T(8,128)}) %all-reduce.3.cloned.1.call-update) | async-done | bytes 524304
  159.0 1.5 constant_dynamic-slice_fusion
Async XLA Ops:
  7.2 48.5 %copy-start = (f32[8,2048]{1,0:T(8,128)S(1)}, f32[8,2048]{1,0:T(8,128)}, u32[]{:S(2)}) copy-start(f32[8,2048]{1,0:T(8,128)} %param.6) | copy-start | bytes 196612
  7.2 48.5 %copy-start.1 = (f32[8,2048]{1,0:T(8,128)S(1)}, f32[8,2048]{1,0:T(8,128)}, u32[]{:S(2)}) copy-start(f32[8,2048]{1,0:T(8,128)} %param.7) | copy-start | bytes 196612
  7.2 48.5 %reduce-scatter.2.cloned.1.call-start = ((), (), s32[]{:S(2)}) async-start(), calls=%async_computation.1 | async-start | bytes 327680 | tf_op jit(solution)/shard_map/reduce_scatter | solution.py:22
  18.3 87.2 %copy-start.2 = (u32[32]{0:T(128)S(1)}, u32[32]{0:T(128)}, u32[]{:S(2)}) copy-start(u32[32]{0:T(128)} %constant.19) | copy-start | bytes 388
  35.3 123.7 %all-reduce.3.cloned.1.call-start = ((), (), s32[]{:S(2)}) async-start(), calls=%async_computation.2 | async-start | bytes 1048576
Sparse Core Ops, SparseCore 0:
  35.4 20.2 reduce-scatter.1
  105.6 53.3 all-reduce.2
where the time goes:
time: 168 us; the launch traced here: 167 us
  waiting for transfers between devices  72.7 us (43%)
  matrix products  51.3 us (31%)
  blocking collectives  24.9 us (15%)
  between operations  14.7 us (9%)
  local copies, waits for them, and re-layouts  2.21 us (1%)
    unnamed x3, waiting for transfers between devices  52.3 us
    dot_general x1, matrix products, body(): lax.dot_general(normed_all, basis, (((1,), (1,)), ((), ())), precision=la...  34.3 us
    reduce_scatter x1, waiting for transfers between devices, body(): lax.psum_scatter(partial_value, 'cols', scatter_dimension=0, tiled=True)  20.4 us
    dot_general x1, matrix products, body(): jnp.dot(gathered.astype(jnp.float32), basis, precision=lax.Precision.HIGH...  16.9 us
    all_gather x1, blocking collectives, body(): normed_all = lax.all_gather(normed, 'cols', axis=0, tiled=True)  13.9 us
    all_gather x1, blocking collectives, body(): gathered = lax.all_gather(gradient, 'rows', axis=0, tiled=True)  11 us
  transfers between devices with their start and end apart: 2, of which 2 were waited for; matrix products, arithmetic and copies ran while one was open for 0% of the time, Pallas kernels for 0%

commit v1 on v0

v1 whole, which is shorter than its diff:
```python
import functools

import jax
import jax.numpy as jnp
from jax import lax
from jax.experimental import pallas as pl
from jax.experimental.pallas import tpu as pltpu
from jax.sharding import PartitionSpec as P

F32, BF16 = jnp.float32, jnp.bfloat16
WHOLE = pl.BlockSpec(memory_space=pltpu.VMEM)
TRANSPOSED = (((1,), (1,)), ((), ()))


def adam_moments(moment, second, rotated):
    moment_new = 0.9 * moment + 0.1 * rotated
    second_new = 0.95 * second + 0.05 * rotated * rotated
    normed = moment_new / (1.0 - 0.9**10) / (jnp.sqrt(second_new / (1.0 - 0.95**10)) + 1e-08)
    return (moment_new, second_new, normed)


def split(x):
    high = x.astype(BF16)
    return high, (x - high.astype(F32)).astype(BF16)


def tile(size, most):
    while size % most:
        most //= 2
    return most


def call(kernel, outs, *args, limit=20 << 20):
    return pl.pallas_call(
        kernel,
        out_shape=outs,
        in_specs=[WHOLE] * len(args),
        out_specs=jax.tree.map(lambda _: WHOLE, outs),
        compiler_params=pltpu.CompilerParams(vmem_limit_bytes=limit),
    )(*args)


def f32(*shape):
    return jax.ShapeDtypeStruct(shape, F32)


def rotate_kernel(g_ref, b_ref, *outs):
    depth, width = b_ref.shape
    rows = g_ref.shape[0] * g_ref.shape[1]
    n = len(outs)
    kt, nt = tile(depth, 1024), tile(width, 256)
    me = lax.axis_index("cols")

    def columns(j, _):
        cs = pl.ds(pl.multiple_of(j * nt, nt), nt)

        def inner(k, total):
            ks = pl.ds(pl.multiple_of(k * kt, kt), kt)
            g = g_ref[:, :, ks].astype(F32).reshape(rows, kt).astype(BF16)
            high, low = split(b_ref[ks, cs])
            return total + jnp.dot(g, high, preferred_element_type=F32) + jnp.dot(g, low, preferred_element_type=F32)

        total = lax.fori_loop(0, depth // kt, inner, jnp.zeros((rows, nt), F32))
        blocks = total.reshape(n, rows // n, nt)
        for s, out in enumerate(outs):
            block = blocks[0]
            for i in range(1, n):
                block = jnp.where(lax.rem(me + s, n) == i, blocks[i], block)
            out[:, cs] = block
        return 0

    lax.fori_loop(0, width // nt, columns, 0)


def moments_kernel(n, m_ref, s_ref, *refs):
    parts, (moment_new, second_new, normed) = refs[:n], refs[n:]
    total = parts[0][...]
    for part in parts[1:]:
        total = total + part[...]
    moment_new[...], second_new[...], normed[...] = adam_moments(m_ref[...], s_ref[...], total)


def back_kernel(n, *refs):
    blocks, b_ref, keep, send, x_ref, o_ref = refs[:n], refs[n], *refs[n + 1 :]
    height, width = b_ref.shape
    rows = x_ref.shape[0]
    each = rows // n
    rt, jt = tile(height, 512), tile(width, 512)
    me = lax.axis_index("cols")
    for s, block in enumerate(blocks):
        x_ref[pl.ds(pl.multiple_of(lax.rem(me - s + n, n) * each, each), each), :] = block[...]

    def out_rows(r, _):
        rs = pl.ds(pl.multiple_of(r * rt, rt), rt)

        def inner(j, total):
            js = pl.ds(pl.multiple_of(j * jt, jt), jt)
            high, low = split(b_ref[rs, js])
            xh, xl = split(x_ref[:, js])
            first = lax.dot_general(jnp.concatenate([xh, xl]), high, TRANSPOSED, preferred_element_type=F32)
            second = lax.dot_general(xh, low, TRANSPOSED, preferred_element_type=F32)
            return total + first[:rows] + first[rows:] + second

        o_ref[:, rs] = lax.fori_loop(0, width // jt, inner, jnp.zeros((rows, rt), F32))
        return 0

    lax.fori_loop(0, height // rt, out_rows, 0)
    pairs, _, four, _ = keep.shape[0], 0, keep.shape[1], 0
    odd = lax.rem(lax.axis_index("rows"), 2) == 1
    whole = o_ref[...].reshape(pairs, 2, four, height)
    keep[...] = jnp.where(odd, whole[:, 1], whole[:, 0])
    send[...] = jnp.where(odd, whole[:, 0], whole[:, 1])


def fold_kernel(keep, got, *outs):
    chips = len(outs)
    chip = lax.axis_index("rows") // 2
    total = keep[...] + got[...]
    for s, out in enumerate(outs):
        block = total[0]
        for i in range(1, chips):
            block = jnp.where(lax.rem(chip + s, chips) == i, total[i], block)
        out[...] = block


def body(gradient, basis, moment, second):
    n, m = lax.axis_size("cols"), lax.axis_size("rows")
    each, width = moment.shape
    four, height = gradient.shape
    held = pltpu.with_memory_space_constraint(basis, pltpu.VMEM)
    gathered = lax.all_gather(gradient, "rows", axis=0)
    parts = call(rotate_kernel, [f32(each, width)] * n, gathered, held)

    def along(x, axis, size, s, step=1):
        pairs = [(i, (i // step + s) % (size // step) * step + i % step) for i in range(size)]
        return lax.ppermute(x, axis, pairs)

    parts = [parts[0]] + [along(parts[s], "cols", n, s) for s in range(1, n)]
    moment_new, second_new, normed = call(
        functools.partial(moments_kernel, n), [f32(each, width)] * 3, moment, second, *parts
    )
    blocks = [normed] + [along(normed, "cols", n, s) for s in range(1, n)]
    chips = m // 2
    keep, send = pl.pallas_call(
        functools.partial(back_kernel, n),
        out_shape=[f32(chips, four, height)] * 2,
        in_specs=[WHOLE] * (n + 1),
        out_specs=[WHOLE] * 2,
        scratch_shapes=[pltpu.VMEM((n * each, width), F32), pltpu.VMEM((m * four, height), F32)],
        compiler_params=pltpu.CompilerParams(vmem_limit_bytes=20 << 20),
    )(*blocks, held)
    got = lax.ppermute(send, "rows", [(i, i ^ 1) for i in range(m)])
    pieces = call(fold_kernel, [f32(four, height)] * chips, keep, got)
    update = pieces[0]
    for s in range(1, chips):
        update = update + along(pieces[s], "rows", m, s, 2)
    return (update, moment_new, second_new)


def solution(mesh):
    placed = (P("rows", "cols"), P("cols", "rows"), P("cols", "rows"), P("cols", "rows"))
    return jax.shard_map(
        body,
        mesh=mesh,
        in_specs=placed,
        out_specs=(P("rows", "cols"), P("cols", "rows"), P("cols", "rows")),
        check_vma=False,
    )
```

time: 168 us -> 84.4 us (0.50)
  waiting for transfers between devices: 72.7 us -> 13.8 us
  matrix products: 51.3 us -> 0 us
  Pallas kernels: 0 us -> 23.4 us
  local copies, waits for them, and re-layouts: 2.21 us -> 21.1 us
  between operations: 14.7 us -> 0.69 us
  blocking collectives: 24.9 us -> 11.1 us
  starting transfers between devices: 0.08 us -> 13.2 us
    unnamed x3 -> x0, waiting for transfers between devices: 52.3 us -> none
    dot_general x2 -> x0, matrix products: 51.3 us -> none  [the longest x1 34.3 us: body(): lax.dot_general(normed_all, basis, (((1,), (1,)), ((), ())), precision=la...]
    pallas_call x0 -> x4, Pallas kernels: none -> 23.4 us  [the longest x1 13.9 us: body(): pl.pallas_call(functools.partial(back_kernel, n), out_shape=[f32(chips, f...]
    reduce_scatter x1 -> x0, waiting for transfers between devices: 20.4 us -> none  [body(): lax.psum_scatter(partial_value, 'cols', scatter_dimension=0, tiled=True)]
    unnamed x9 -> x8, local copies, waits for them, and re-layouts: 2.21 us -> 21.1 us
    ppermute x0 -> x10, waiting for transfers between devices: none -> 13.8 us  [the longest x9 12.3 us: along(): return lax.ppermute(x, axis, pairs)]
    all_gather x2 -> x1, blocking collectives: 24.9 us -> 11.1 us  [body(): gathered = lax.all_gather(gradient, 'rows', axis=0)]
    ppermute x0 -> x10, starting transfers between devices: none -> 13.2 us  [the longest x9 13.1 us: along(): return lax.ppermute(x, axis, pairs)]
  transfers between devices with their start and end apart: 2 -> 10, of which waited for: 2 -> 8; matrix products, arithmetic and copies ran while one was open for 0% -> 0% of each run, Pallas kernels for 0% -> 0%
where the time goes in v1:
time: 84.4 us; the launch traced here: 84 us
  Pallas kernels  23.4 us (28%)
  local copies, waits for them, and re-layouts  21.1 us (25%)
  waiting for transfers between devices  13.8 us (16%)
  starting transfers between devices  13.2 us (16%)
  blocking collectives  11.1 us (13%)
    unnamed x8, local copies, waits for them, and re-layouts  21.1 us
    pallas_call x1, Pallas kernels, body(): pl.pallas_call(functools.partial(back_kernel, n), out_shape=[f32(chips, f...  13.9 us
    ppermute x9, starting transfers between devices, along(): return lax.ppermute(x, axis, pairs)  13.1 us
    ppermute x9, waiting for transfers between devices, along(): return lax.ppermute(x, axis, pairs)  12.3 us
    all_gather x1, blocking collectives, body(): gathered = lax.all_gather(gradient, 'rows', axis=0)  11.1 us
    pallas_call x3, Pallas kernels, call(): pl.pallas_call(kernel, out_shape=outs, in_specs=[WHOLE] * len(args), out_...  9.51 us
  transfers between devices with their start and end apart: 10, of which 8 were waited for; matrix products, arithmetic and copies ran while one was open for 0% of the time, Pallas kernels for 0%

profile of v1, /device:TPU:0, one launch (start us, length us, event | category | flops | bytes accessed | tf_op | source)
XLA Modules:
  0.0 84.0 jit_solution(6949779397745187605)
XLA Ops:
  0.6 0.0 copy-start.3
  0.6 0.0 copy-start.2
  0.7 11.1 %all-gather.1.g_ref = bf16[8,4,4096]{2,1,0:T(4,128)(2,1)S(1)} all-gather(bf16[1,4,4096]{2,1,0:T(4,128)(2,1)} %bitcast.1), channel_id=2, replica_groups=mesh['rows'=8,'cols'=4] {'rows'}, dimensions={0}, use_global_device_ids=true | all-gather | bytes 294912 | tf_op jit(solution)/shard_map/all_gather | solution.py:131
  11.8 10.5 %copy-done = f32[4096,2048]{1,0:T(8,128)S(1)} copy-done((f32[4096,2048]{1,0:T(8,128)S(1)}, f32[4096,2048]{1,0:T(8,128)}, u32[]{:S(2)}) %copy-start) | copy-done | bytes 33554456
  22.3 8.8 %shard_map.67 = (f32[8,2048]{1,0:T(8,128)S(1)}, f32[8,2048]{1,0:T(8,128)S(1)}, f32[8,2048]{1,0:T(8,128)S(1)}, f32[8,2048]{1,0:T(8,128)S(1)}) custom-call(bf16[8,4,4096]{2,1,0:T(4,128)(2,1)S(1)} %all-gather.1.g_ref, f32[4096,2048]{1,0:T(8,128)S(1)} %copy-done), custom_call_target="tpu_custom_call" | custom-call | tf_op jit(solution)/shard_map/pallas_call | solution.py:34
  31.1 1.6 %collective-permute-start = (f32[8,2048]{1,0:T(8,128)S(1)}, f32[8,2048]{1,0:T(8,128)S(1)}, u32[]{:S(2)}, u32[]{:S(2)}) collective-permute-start(f32[8,2048]{1,0:T(8,128)S(1)} %get-tuple-element.17), channel_id=1, source_target_pairs={{0,1},{1,2},{2,3},{3,0},{4,5},{5,6},{6,7},{7,4},{8,9},{9,10},{10,1... | collective-permute-start | bytes 196616 | tf_op jit(solution)/shard_map/ppermute | solution.py:136
  32.8 2.6 %collective-permute-start.1 = (f32[8,2048]{1,0:T(8,128)S(1)}, f32[8,2048]{1,0:T(8,128)S(1)}, u32[]{:S(2)}, u32[]{:S(2)}) collective-permute-start(f32[8,2048]{1,0:T(8,128)S(1)} %get-tuple-element.18), channel_id=1, source_target_pairs={{0,2},{1,3},{2,0},{3,1},{4,6},{5,7},{6,4},{7,5},{8,10},{9,11},{10,... | collective-permute-start | bytes 196616 | tf_op jit(solution)/shard_map/ppermute | solution.py:136
  35.3 1.3 %collective-permute-start.2 = (f32[8,2048]{1,0:T(8,128)S(1)}, f32[8,2048]{1,0:T(8,128)S(1)}, u32[]{:S(2)}, u32[]{:S(2)}) collective-permute-start(f32[8,2048]{1,0:T(8,128)S(1)} %get-tuple-element.19), channel_id=1, source_target_pairs={{0,3},{1,0},{2,1},{3,2},{4,7},{5,4},{6,5},{7,6},{8,11},{9,8},{10,9... | collective-permute-start | bytes 196616 | tf_op jit(solution)/shard_map/ppermute | solution.py:136
  36.7 0.8 collective-permute-done.refs_1_
  37.5 2.7 %collective-permute-done.1.refs_2_ = f32[8,2048]{1,0:T(8,128)S(1)} collective-permute-done((f32[8,2048]{1,0:T(8,128)S(1)}, f32[8,2048]{1,0:T(8,128)S(1)}, u32[]{:S(2)}, u32[]{:S(2)}) %collective-permute-start.1) | collective-permute-done | bytes 65568 | tf_op jit(solution)/shard_map/ppermute | solution.py:136
  40.3 0.3 collective-permute-done.2.refs_3_
  40.5 0.0 copy-done.3
  40.5 0.0 copy-done.2
  40.5 0.7 shard_map.68
  41.2 2.7 %collective-permute-start.5 = (f32[8,2048]{1,0:T(8,128)S(1)}, f32[8,2048]{1,0:T(8,128)S(1)}, u32[]{:S(2)}, u32[]{:S(2)}) collective-permute-start(f32[8,2048]{1,0:T(8,128)S(1)} %get-tuple-element.20.refs_0_), channel_id=1, source_target_pairs={{0,3},{1,0},{2,1},{3,2},{4,7},{5,4},{6,5},{7,6},{8,11},{9,8},{10,9... | collective-permute-start | bytes 196616 | tf_op jit(solution)/shard_map/ppermute | solution.py:136
  43.9 0.4 collective-permute-start.4
  44.3 0.2 collective-permute-start.3
  44.5 1.8 %collective-permute-done.5.refs_3_ = f32[8,2048]{1,0:T(8,128)S(1)} collective-permute-done((f32[8,2048]{1,0:T(8,128)S(1)}, f32[8,2048]{1,0:T(8,128)S(1)}, u32[]{:S(2)}, u32[]{:S(2)}) %collective-permute-start.5) | collective-permute-done | bytes 65568 | tf_op jit(solution)/shard_map/ppermute | solution.py:136
  46.3 4.5 %collective-permute-done.4.refs_2_ = f32[8,2048]{1,0:T(8,128)S(1)} collective-permute-done((f32[8,2048]{1,0:T(8,128)S(1)}, f32[8,2048]{1,0:T(8,128)S(1)}, u32[]{:S(2)}, u32[]{:S(2)}) %collective-permute-start.4) | collective-permute-done | bytes 65568 | tf_op jit(solution)/shard_map/ppermute | solution.py:136
  50.7 0.0 collective-permute-done.3.refs_1_
  50.7 10.5 %copy-done.1 = f32[4096,2048]{1,0:T(8,128)S(1)} copy-done((f32[4096,2048]{1,0:T(8,128)S(1)}, f32[4096,2048]{1,0:T(8,128)}, u32[]{:S(2)}) %copy-start.1) | copy-done | bytes 33554456
  61.3 13.9 %shard_map.69 = (f32[4,4,4096]{2,1,0:T(4,128)S(1)}, f32[4,4,4096]{2,1,0:T(4,128)S(1)}) custom-call(f32[8,2048]{1,0:T(8,128)S(1)} %get-tuple-element.20.refs_0_, f32[8,2048]{1,0:T(8,128)S(1)} %collective-permute-done.3.refs_1_, f32[8,2048]{1,0:T(8,128)S(1)} %collective-permute-done.4.refs_2_, f32[8,2048]{1,0:T(8,128)S(1)} %collective-permute-done.5.refs_3_, ...), custom_call_target="tpu_custom_call" | custom-call | tf_op jit(solution)/shard_map/pallas_call | solution.py:144
  75.2 0.1 collective-permute-start.6
  75.3 1.5 %collective-permute-done.6.got = f32[4,4,4096]{2,1,0:T(4,128)S(1)} collective-permute-done((f32[4,4,4096]{2,1,0:T(4,128)S(1)}, f32[4,4,4096]{2,1,0:T(4,128)S(1)}, u32[]{:S(2)}, u32[]{:S(2)}) %collective-permute-start.6) | collective-permute-done | bytes 262176 | tf_op jit(solution)/shard_map/ppermute | solution.py:152
  76.8 0.1 shard_map.70
  76.9 1.3 %collective-permute-start.7 = (f32[4,4096]{1,0:T(4,128)S(1)}, f32[4,4096]{1,0:T(4,128)S(1)}, u32[]{:S(2)}, u32[]{:S(2)}) collective-permute-start(f32[4,4096]{1,0:T(4,128)S(1)} %get-tuple-element.24), channel_id=1, source_target_pairs={{0,8},{4,12},{8,16},{12,20},{16,24},{20,28},{24,0},{28,4},{1,9},{5... | collective-permute-start | bytes 196616 | tf_op jit(solution)/shard_map/ppermute | solution.py:136
  78.2 0.8 collective-permute-start.8
  79.0 2.2 %collective-permute-start.9 = (f32[4,4096]{1,0:T(4,128)S(1)}, f32[4,4096]{1,0:T(4,128)S(1)}, u32[]{:S(2)}, u32[]{:S(2)}) collective-permute-start(f32[4,4096]{1,0:T(4,128)S(1)} %get-tuple-element.26), channel_id=1, source_target_pairs={{0,24},{4,28},{8,0},{12,4},{16,8},{20,12},{24,16},{28,20},{1,25},{... | collective-permute-start | bytes 196616 | tf_op jit(solution)/shard_map/ppermute | solution.py:136
  81.1 1.2 %collective-permute-done.7 = f32[4,4096]{1,0:T(4,128)S(1)} collective-permute-done((f32[4,4096]{1,0:T(4,128)S(1)}, f32[4,4096]{1,0:T(4,128)S(1)}, u32[]{:S(2)}, u32[]{:S(2)}) %collective-permute-start.7) | collective-permute-done | bytes 65568 | tf_op jit(solution)/shard_map/ppermute | solution.py:136
  82.3 1.0 %collective-permute-done.8 = f32[4,4096]{1,0:T(4,128)S(1)} collective-permute-done((f32[4,4096]{1,0:T(4,128)S(1)}, f32[4,4096]{1,0:T(4,128)S(1)}, u32[]{:S(2)}, u32[]{:S(2)}) %collective-permute-start.8) | collective-permute-done | bytes 65568 | tf_op jit(solution)/shard_map/ppermute | solution.py:136
  83.4 0.0 collective-permute-done.9
  83.4 0.7 add_add_fusion
  (2 shorter events, 0.0 us)
Async XLA Ops:
  0.6 39.9 %copy-start.3 = (f32[8,2048]{1,0:T(8,128)S(1)}, f32[8,2048]{1,0:T(8,128)}, u32[]{:S(2)}) copy-start(f32[8,2048]{1,0:T(8,128)} %s_ref.1) | copy-start | bytes 196612
  0.6 39.9 %copy-start.2 = (f32[8,2048]{1,0:T(8,128)S(1)}, f32[8,2048]{1,0:T(8,128)}, u32[]{:S(2)}) copy-start(f32[8,2048]{1,0:T(8,128)} %m_ref.1) | copy-start | bytes 196612
  11.8 10.5 %copy-start = (f32[4096,2048]{1,0:T(8,128)S(1)}, f32[4096,2048]{1,0:T(8,128)}, u32[]{:S(2)}) copy-start(f32[4096,2048]{1,0:T(8,128)} %refs_4_.1) | copy-start | bytes 100663296
  31.1 6.4 %collective-permute-start = (f32[8,2048]{1,0:T(8,128)S(1)}, f32[8,2048]{1,0:T(8,128)S(1)}, u32[]{:S(2)}, u32[]{:S(2)}) collective-permute-start(f32[8,2048]{1,0:T(8,128)S(1)} %get-tuple-element.17), channel_id=1, source_target_pairs={{0,1},{1,2},{2,3},{3,0},{4,5},{5,6},{6,7},{7,4},{8,9},{9,10},{10,1... | collective-permute-start | bytes 196616 | tf_op jit(solution)/shard_map/ppermute | solution.py:136
  32.8 7.5 %collective-permute-start.1 = (f32[8,2048]{1,0:T(8,128)S(1)}, f32[8,2048]{1,0:T(8,128)S(1)}, u32[]{:S(2)}, u32[]{:S(2)}) collective-permute-start(f32[8,2048]{1,0:T(8,128)S(1)} %get-tuple-element.18), channel_id=1, source_target_pairs={{0,2},{1,3},{2,0},{3,1},{4,6},{5,7},{6,4},{7,5},{8,10},{9,11},{10,... | collective-permute-start | bytes 196616 | tf_op jit(solution)/shard_map/ppermute | solution.py:136
  35.3 5.2 %collective-permute-start.2 = (f32[8,2048]{1,0:T(8,128)S(1)}, f32[8,2048]{1,0:T(8,128)S(1)}, u32[]{:S(2)}, u32[]{:S(2)}) collective-permute-start(f32[8,2048]{1,0:T(8,128)S(1)} %get-tuple-element.19), channel_id=1, source_target_pairs={{0,3},{1,0},{2,1},{3,2},{4,7},{5,4},{6,5},{7,6},{8,11},{9,8},{10,9... | collective-permute-start | bytes 196616 | tf_op jit(solution)/shard_map/ppermute | solution.py:136
  41.2 5.1 %collective-permute-start.5 = (f32[8,2048]{1,0:T(8,128)S(1)}, f32[8,2048]{1,0:T(8,128)S(1)}, u32[]{:S(2)}, u32[]{:S(2)}) collective-permute-start(f32[8,2048]{1,0:T(8,128)S(1)} %get-tuple-element.20.refs_0_), channel_id=1, source_target_pairs={{0,3},{1,0},{2,1},{3,2},{4,7},{5,4},{6,5},{7,6},{8,11},{9,8},{10,9... | collective-permute-start | bytes 196616 | tf_op jit(solution)/shard_map/ppermute | solution.py:136
  43.9 6.8 %collective-permute-start.4 = (f32[8,2048]{1,0:T(8,128)S(1)}, f32[8,2048]{1,0:T(8,128)S(1)}, u32[]{:S(2)}, u32[]{:S(2)}) collective-permute-start(f32[8,2048]{1,0:T(8,128)S(1)} %get-tuple-element.20.refs_0_), channel_id=1, source_target_pairs={{0,2},{1,3},{2,0},{3,1},{4,6},{5,7},{6,4},{7,5},{8,10},{9,11},{10,... | collective-permute-start | bytes 196616 | tf_op jit(solution)/shard_map/ppermute | solution.py:136
  44.3 6.4 %collective-permute-start.3 = (f32[8,2048]{1,0:T(8,128)S(1)}, f32[8,2048]{1,0:T(8,128)S(1)}, u32[]{:S(2)}, u32[]{:S(2)}) collective-permute-start(f32[8,2048]{1,0:T(8,128)S(1)} %get-tuple-element.20.refs_0_), channel_id=1, source_target_pairs={{0,1},{1,2},{2,3},{3,0},{4,5},{5,6},{6,7},{7,4},{8,9},{9,10},{10,1... | collective-permute-start | bytes 196616 | tf_op jit(solution)/shard_map/ppermute | solution.py:136
  50.7 10.5 %copy-start.1 = (f32[4096,2048]{1,0:T(8,128)S(1)}, f32[4096,2048]{1,0:T(8,128)}, u32[]{:S(2)}) copy-start(f32[4096,2048]{1,0:T(8,128)} %refs_4_.1) | copy-start | bytes 100663296
  75.2 1.6 %collective-permute-start.6 = (f32[4,4,4096]{2,1,0:T(4,128)S(1)}, f32[4,4,4096]{2,1,0:T(4,128)S(1)}, u32[]{:S(2)}, u32[]{:S(2)}) collective-permute-start(f32[4,4,4096]{2,1,0:T(4,128)S(1)} %get-tuple-element.22), channel_id=1, source_target_pairs={{0,4},{4,0},{8,12},{12,8},{16,20},{20,16},{24,28},{28,24},{1,5},{5... | collective-permute-start | bytes 786440 | tf_op jit(solution)/shard_map/ppermute | solution.py:152
  76.9 5.5 %collective-permute-start.7 = (f32[4,4096]{1,0:T(4,128)S(1)}, f32[4,4096]{1,0:T(4,128)S(1)}, u32[]{:S(2)}, u32[]{:S(2)}) collective-permute-start(f32[4,4096]{1,0:T(4,128)S(1)} %get-tuple-element.24), channel_id=1, source_target_pairs={{0,8},{4,12},{8,16},{12,20},{16,24},{20,28},{24,0},{28,4},{1,9},{5... | collective-permute-start | bytes 196616 | tf_op jit(solution)/shard_map/ppermute | solution.py:136
  78.2 5.2 %collective-permute-start.8 = (f32[4,4096]{1,0:T(4,128)S(1)}, f32[4,4096]{1,0:T(4,128)S(1)}, u32[]{:S(2)}, u32[]{:S(2)}) collective-permute-start(f32[4,4096]{1,0:T(4,128)S(1)} %get-tuple-element.25), channel_id=1, source_target_pairs={{0,16},{4,20},{8,24},{12,28},{16,0},{20,4},{24,8},{28,12},{1,17},{... | collective-permute-start | bytes 196616 | tf_op jit(solution)/shard_map/ppermute | solution.py:136
  79.0 4.4 %collective-permute-start.9 = (f32[4,4096]{1,0:T(4,128)S(1)}, f32[4,4096]{1,0:T(4,128)S(1)}, u32[]{:S(2)}, u32[]{:S(2)}) collective-permute-start(f32[4,4096]{1,0:T(4,128)S(1)} %get-tuple-element.26), channel_id=1, source_target_pairs={{0,24},{4,28},{8,0},{12,4},{16,8},{20,12},{24,16},{28,20},{1,25},{... | collective-permute-start | bytes 196616 | tf_op jit(solution)/shard_map/ppermute | solution.py:136

commit v2 on v0

v2 whole, which is shorter than its diff:
```python
import functools

import jax
import jax.numpy as jnp
from jax import lax
from jax.experimental import pallas as pl
from jax.experimental.pallas import tpu as pltpu
from jax.sharding import PartitionSpec as P

F32, BF16 = jnp.float32, jnp.bfloat16
WHOLE = pl.BlockSpec(memory_space=pltpu.VMEM)
FAR = pl.BlockSpec(memory_space=pltpu.HBM)
ANY = pl.BlockSpec(memory_space=pl.ANY)
TRANSPOSED = (((1,), (1,)), ((), ()))
MIB = 1 << 20
SHARES = (2, 1, 5)
BUFFERS = 3


def f32(*shape):
    return jax.ShapeDtypeStruct(shape, F32)


def cost(moved, flops=0):
    return pl.CostEstimate(flops=flops, bytes_accessed=moved, transcendentals=0)


def params(mib):
    return pltpu.CompilerParams(vmem_limit_bytes=mib * MIB)


def adam_moments(moment, second, rotated):
    moment_new = 0.9 * moment + 0.1 * rotated
    second_new = 0.95 * second + 0.05 * rotated * rotated
    normed = moment_new / (1.0 - 0.9**10) / (jnp.sqrt(second_new / (1.0 - 0.95**10)) + 1e-08)
    return (moment_new, second_new, normed)


def split(x):
    high = x.astype(BF16)
    return high, (x - high.astype(F32)).astype(BF16)


def load_kernel(first, count, after, *refs):
    b_ref, high_ref, low_ref, buf, sems = refs[after:]
    depth, rows, _ = buf.shape

    def copy(i):
        at = pl.ds(pl.multiple_of((first + i) * rows, rows), rows)
        return pltpu.make_async_copy(b_ref.at[at, :], buf.at[lax.rem(i, depth)], sems.at[lax.rem(i, depth)])

    for i in range(depth):
        copy(i).start()

    def step(i, _):
        copy(i).wait()
        at = pl.ds(pl.multiple_of(i * rows, rows), rows)
        high_ref[at, :], low_ref[at, :] = split(buf[lax.rem(i, depth)])

        @pl.when(i + depth < count)
        def _():
            copy(i + depth).start()

        return 0

    lax.fori_loop(0, count, step, 0)


def load(basis, first, count, tile, *after):
    width = basis.shape[1]
    depth = min(count, BUFFERS)
    return list(
        pl.pallas_call(
            functools.partial(load_kernel, first, count, len(after)),
            out_shape=[pltpu.VMEM((count * tile, width), BF16)] * 2,
            in_specs=[ANY] * len(after) + [FAR],
            out_specs=[WHOLE] * 2,
            scratch_shapes=[pltpu.VMEM((depth, tile, width), F32), pltpu.SemaphoreType.DMA((depth,))],
            cost_estimate=cost(count * tile * width * 8),
            compiler_params=params(8),
        )(*after, basis)
    )


def pack_kernel(*refs):
    _, *parts, out = refs
    for i, part in enumerate(parts):
        out[i] = part[...]


def rotate_kernel(n, kept, own_ref, got_ref, *refs):
    pieces, b_ref, (*outs, rest), (g_ref, total, sems) = (
        refs[:kept], refs[kept], refs[kept + 1 : kept + n + 2], refs[kept + n + 2 :]
    )
    steps, (depth, width) = sems.shape[0], rest.shape
    rows = depth // steps
    first = sum(high.shape[0] for high in pieces[::2])
    columns = min(width, 256)

    def copy(i):
        from_row, to_row = (pl.multiple_of(x, rows) for x in (first + i * rows, i * rows))
        return pltpu.make_async_copy(b_ref.at[pl.ds(from_row, rows), :], rest.at[pl.ds(to_row, rows), :], sems.at[i])

    for i in range(steps):
        copy(i).start()
    even = lax.rem(lax.axis_index("rows"), 2) == 0
    own, got = own_ref[...].astype(F32), got_ref[...].astype(F32)
    both = jnp.concatenate([jnp.where(even, own, got), jnp.where(even, got, own)], axis=1)
    g_ref[...] = both.reshape(g_ref.shape).astype(BF16)
    total[...] = jnp.zeros_like(total)

    def add(row, take):
        g = g_ref[:, pl.ds(pl.multiple_of(row, rows), rows)]
        for j in range(width // columns):
            at = slice(j * columns, (j + 1) * columns)
            high, low = take(at)
            total[:, at] += jnp.dot(g, high, preferred_element_type=F32) + jnp.dot(g, low, preferred_element_type=F32)

    done = 0
    for high, low in zip(pieces[::2], pieces[1::2]):

        def step(i, _, high=high, low=low, done=done):
            at = pl.ds(pl.multiple_of(i * rows, rows), rows)
            add(done + i * rows, lambda cs: (high[at, cs], low[at, cs]))
            return 0

        lax.fori_loop(0, high.shape[0] // rows, step, 0)
        done += high.shape[0]

    def step(i, _):
        copy(i).wait()
        at = pl.ds(pl.multiple_of(i * rows, rows), rows)
        add(first + i * rows, lambda cs: split(rest[at, cs]))
        return 0

    lax.fori_loop(0, steps, step, 0)
    chips, pair = own_ref.shape[0], 2 * own_ref.shape[1]
    chip = lax.axis_index("rows") // 2
    each = chips // n
    for s, out in enumerate(outs):
        place = (lax.axis_index("cols") ^ s) * each
        for i in range(each):
            slot = chip ^ (place + i)
            out[i * pair : (i + 1) * pair, :] = total[pl.ds(pl.multiple_of(slot * pair, pair), pair), :]


def moments_kernel(n, m_ref, s_ref, *refs):
    parts, (moment_new, second_new, normed) = refs[:n], refs[-3:]
    total = parts[0][...]
    for part in parts[1:]:
        total = total + part[...]
    moment_new[...], second_new[...], normed[...] = adam_moments(m_ref[...], s_ref[...], total)


def back_kernel(n, kept, *refs):
    blocks, pieces, (keep, send, x_ref, x2_ref, o_ref) = refs[:n], refs[n : n + kept], refs[n + kept :]
    each, rows = blocks[0].shape[0], x_ref.shape[0]
    for s, block in enumerate(blocks):
        place = (lax.axis_index("cols") ^ s) * each
        x_ref[pl.ds(pl.multiple_of(place, each), each), :] = block[...]
    high, low = split(x_ref[...])
    x2_ref[:rows, :], x2_ref[rows:, :] = high, low
    *pieces, rest = pieces
    done = 0

    def products(size, block, take):
        def step(i, _):
            high, low = take(pl.ds(pl.multiple_of(i * block, block), block))
            first = lax.dot_general(x2_ref[...], high, TRANSPOSED, preferred_element_type=F32)
            second = lax.dot_general(x2_ref[:rows, :], low, TRANSPOSED, preferred_element_type=F32)
            to = pl.ds(pl.multiple_of(done + i * block, 128), block)
            o_ref[:, to] = first[:rows] + first[rows:] + second
            return 0

        lax.fori_loop(0, size // block, step, 0)
        return size

    for high, low in zip(pieces[::2], pieces[1::2]):
        size = high.shape[0]
        done += products(size, min(size, 1024), lambda at: (high[at, :], low[at, :]))
    products(rest.shape[0], o_ref.shape[1] // 8, lambda at: split(rest[at, :]))
    odd = lax.rem(lax.axis_index("rows"), 2) == 1
    chips, four, height = keep.shape
    whole = o_ref[...].reshape(chips, 2, four, height)
    keep[...] = jnp.where(odd, whole[:, 1], whole[:, 0])
    send[...] = jnp.where(odd, whole[:, 0], whole[:, 1])


def fold_kernel(keep, got, *outs):
    chip = lax.axis_index("rows") // 2
    total = keep[...] + got[...]
    for s, out in enumerate(outs):
        block = total[0]
        for i in range(1, len(outs)):
            block = jnp.where((chip ^ s) == i, total[i], block)
        out[...] = block


def body(gradient, basis, moment, second):
    n, m = lax.axis_size("cols"), lax.axis_size("rows")
    chips = m // 2
    each, width = moment.shape
    four, height = gradient.shape
    tile = height // 16
    basis = pltpu.with_memory_space_constraint(basis, pltpu.HBM)

    def along_rows(x, s):
        return lax.ppermute(x, "rows", [(i, i ^ s) for i in range(m)])

    def along_cols(x, s):
        return lax.ppermute(x, "cols", [(i, i ^ s) for i in range(n)])

    from_chips = [gradient] + [along_rows(gradient, 2 * s) for s in range(1, chips)]
    pieces = load(basis, 0, 2 * SHARES[0], tile)
    own = pl.pallas_call(
        pack_kernel,
        out_shape=jax.ShapeDtypeStruct((chips, four, height), BF16),
        in_specs=[ANY] + [WHOLE] * chips,
        out_specs=WHOLE,
        compiler_params=params(4),
    )(pieces[0], *from_chips)
    got = along_rows(own, 1)
    pieces = pieces + load(basis, 2 * SHARES[0], 2 * SHARES[1], tile, own)
    *parts, rest = pl.pallas_call(
        functools.partial(rotate_kernel, n, len(pieces)),
        out_shape=[f32(each, width)] * n + [pltpu.VMEM((SHARES[2] * height // 8, width), F32)],
        in_specs=[WHOLE] * (len(pieces) + 2) + [FAR],
        out_specs=[WHOLE] * (n + 1),
        scratch_shapes=[
            pltpu.VMEM((n * each, height), BF16),
            pltpu.VMEM((n * each, width), F32),
            pltpu.SemaphoreType.DMA((SHARES[2],)),
        ],
        cost_estimate=cost(height * width * 4),
        compiler_params=params(8),
    )(own, got, *pieces, basis)
    pieces = [pltpu.with_memory_space_constraint(x, pltpu.VMEM) for x in pieces + [rest]]
    parts = [parts[0]] + [along_cols(parts[s], s) for s in range(1, n)]
    moment_new, second_new, normed = pl.pallas_call(
        functools.partial(moments_kernel, n),
        out_shape=[f32(each, width)] * 3,
        in_specs=[WHOLE] * (n + 2) + [WHOLE] * len(pieces),
        out_specs=[WHOLE] * 3,
        compiler_params=params(4),
    )(moment, second, *parts, *pieces)
    blocks = [normed] + [along_cols(normed, s) for s in range(1, n)]
    keep, send = pl.pallas_call(
        functools.partial(back_kernel, n, len(pieces)),
        out_shape=[f32(chips, four, height)] * 2,
        in_specs=[WHOLE] * (n + len(pieces)),
        out_specs=[WHOLE] * 2,
        scratch_shapes=[
            pltpu.VMEM((n * each, width), F32),
            pltpu.VMEM((2 * n * each, width), BF16),
            pltpu.VMEM((n * each, height), F32),
        ],
        cost_estimate=cost(height * width * 4),
        compiler_params=params(8),
    )(*blocks, *pieces)
    got = along_rows(send, 1)
    pieces = pl.pallas_call(
        fold_kernel,
        out_shape=[f32(four, height)] * chips,
        in_specs=[WHOLE] * 2,
        out_specs=[WHOLE] * chips,
        compiler_params=params(8),
    )(keep, got)
    update = pieces[0]
    for s in range(1, chips):
        update = update + along_rows(pieces[s], 2 * s)
    return (update, moment_new, second_new)


def solution(mesh):
    placed = (P("rows", "cols"), P("cols", "rows"), P("cols", "rows"), P("cols", "rows"))
    return jax.shard_map(
        body,
        mesh=mesh,
        in_specs=placed,
        out_specs=(P("rows", "cols"), P("cols", "rows"), P("cols", "rows")),
        check_vma=False,
    )
```

time: 168 us -> 61.5 us (0.37)
  waiting for transfers between devices: 72.7 us -> 16.7 us
  matrix products: 51.3 us -> 0 us
  Pallas kernels: 0 us -> 26.1 us
  blocking collectives: 24.9 us -> 0 us
  starting transfers between devices: 0.08 us -> 17.1 us
  between operations: 14.7 us -> 0.75 us
  local copies, waits for them, and re-layouts: 2.21 us -> 0.02 us
    unnamed x3 -> x0, waiting for transfers between devices: 52.3 us -> none
    dot_general x2 -> x0, matrix products: 51.3 us -> none  [the longest x1 34.3 us: body(): lax.dot_general(normed_all, basis, (((1,), (1,)), ((), ())), precision=la...]
    pallas_call x0 -> x7, Pallas kernels: none -> 26.1 us  [the longest x1 10.8 us: body(): pl.pallas_call(functools.partial(back_kernel, n, len(pieces)), out_shape=...]
    all_gather x2 -> x0, blocking collectives: 24.9 us -> none  [the longest x1 13.9 us: body(): normed_all = lax.all_gather(normed, 'cols', axis=0, tiled=True)]
    reduce_scatter x1 -> x0, waiting for transfers between devices: 20.4 us -> none  [body(): lax.psum_scatter(partial_value, 'cols', scatter_dimension=0, tiled=True)]
    ppermute x0 -> x14, starting transfers between devices: none -> 17.1 us  [the longest x6 8.84 us: along_cols(): return lax.ppermute(x, 'cols', [(i, i ^ s) for i in range(n)])]
    ppermute x0 -> x14, waiting for transfers between devices: none -> 16.7 us  [the longest x6 10.1 us: along_cols(): return lax.ppermute(x, 'cols', [(i, i ^ s) for i in range(n)])]
    unnamed x9 -> x6, local copies, waits for them, and re-layouts: 2.21 us -> 0.02 us
  transfers between devices with their start and end apart: 2 -> 14, of which waited for: 2 -> 10; matrix products, arithmetic and copies ran while one was open for 0% -> 0% of each run, Pallas kernels for 0% -> 11%
where the time goes in v2:
time: 61.5 us; the launch traced here: 61.4 us
  Pallas kernels  26.1 us (42%)
  starting transfers between devices  17.1 us (28%)
  waiting for transfers between devices  16.7 us (27%)
  between operations  0.75 us (1%)
  other arithmetic  0.66 us (1%)
    pallas_call x1, Pallas kernels, body(): pl.pallas_call(functools.partial(back_kernel, n, len(pieces)), out_shape=...  10.8 us
    ppermute x6, waiting for transfers between devices, along_cols(): return lax.ppermute(x, 'cols', [(i, i ^ s) for i in range(n)])  10.1 us
    ppermute x6, starting transfers between devices, along_cols(): return lax.ppermute(x, 'cols', [(i, i ^ s) for i in range(n)])  8.84 us
    ppermute x8, starting transfers between devices, along_rows(): return lax.ppermute(x, 'rows', [(i, i ^ s) for i in range(m)])  8.3 us
    pallas_call x1, Pallas kernels, body(): pl.pallas_call(functools.partial(rotate_kernel, n, len(pieces)), out_shap...  8.03 us
    ppermute x8, waiting for transfers between devices, along_rows(): return lax.ppermute(x, 'rows', [(i, i ^ s) for i in range(m)])  6.67 us
    pallas_call x2, Pallas kernels, load(): pl.pallas_call(functools.partial(load_kernel, first, count, len(after)),...  6.58 us
  transfers between devices with their start and end apart: 14, of which 10 were waited for; matrix products, arithmetic and copies ran while one was open for 0% of the time, Pallas kernels for 11%

profile of v2, /device:TPU:0, one launch (start us, length us, event | category | flops | bytes accessed | tf_op | source)
XLA Modules:
  0.0 61.4 jit_solution(9886174247272005076)
XLA Ops:
  0.6 3.1 %collective-permute-start.1 = (bf16[4,4096]{1,0:T(4,128)(2,1)}, bf16[4,4096]{1,0:T(4,128)(2,1)S(1)}, u32[]{:S(2)}, u32[]{:S(2)}) collective-permute-start(bf16[4,4096]{1,0:T(4,128)(2,1)} %refs_1_.2), channel_id=1, source_target_pairs={{0,16},{4,20},{8,24},{12,28},{16,0},{20,4},{24,8},{28,12},{1,17},{... | collective-permute-start | bytes 98312 | tf_op jit(solution)/shard_map/ppermute | solution.py:208
  3.7 1.5 %collective-permute-start = (bf16[4,4096]{1,0:T(4,128)(2,1)}, bf16[4,4096]{1,0:T(4,128)(2,1)S(1)}, u32[]{:S(2)}, u32[]{:S(2)}) collective-permute-start(bf16[4,4096]{1,0:T(4,128)(2,1)} %refs_1_.2), channel_id=1, source_target_pairs={{0,8},{4,12},{8,0},{12,4},{16,24},{20,28},{24,16},{28,20},{1,9},{5... | collective-permute-start | bytes 98312 | tf_op jit(solution)/shard_map/ppermute | solution.py:208
  5.2 0.0 collective-permute-start.2
  5.2 4.0 %shard_map.67 = (bf16[1024,2048]{1,0:T(8,128)(2,1)S(1)}, bf16[1024,2048]{1,0:T(8,128)(2,1)S(1)}) custom-call(f32[4096,2048]{1,0:T(8,128)} %refs_4_.1), custom_call_target="tpu_custom_call" | custom-call | bytes 16777216 | tf_op jit(solution)/shard_map/pallas_call | solution.py:73
  9.3 0.9 %collective-permute-done.2.refs_4_ = bf16[4,4096]{1,0:T(4,128)(2,1)S(1)} collective-permute-done((bf16[4,4096]{1,0:T(4,128)(2,1)}, bf16[4,4096]{1,0:T(4,128)(2,1)S(1)}, u32[]{:S(2)}, u32[]{:S(2)}) %collective-permute-start.2) | collective-permute-done | bytes 32800 | tf_op jit(solution)/shard_map/ppermute | solution.py:208
  10.2 0.1 collective-permute-start.3
  10.3 2.5 %shard_map.69 = (bf16[512,2048]{1,0:T(8,128)(2,1)S(1)}, bf16[512,2048]{1,0:T(8,128)(2,1)S(1)}) custom-call(bf16[4,4,4096]{2,1,0:T(4,128)(2,1)S(1)} %shard_map.68.refs_0_.own_ref, f32[4096,2048]{1,0:T(8,128)} %refs_4_.1), custom_call_target="tpu_custom_call" | custom-call | bytes 8388608 | tf_op jit(solution)/shard_map/pallas_call | solution.py:73
  12.9 0.0 copy-start
  12.9 8.0 %shard_map.70 = (f32[8,2048]{1,0:T(8,128)S(1)}, f32[8,2048]{1,0:T(8,128)S(1)}, f32[8,2048]{1,0:T(8,128)S(1)}, f32[8,2048]{1,0:T(8,128)S(1)}, f32[2560,2048]{1,0:T(8,128)S(1)}) custom-call(bf16[4,4,4096]{2,1,0:T(4,128)(2,1)S(1)} %shard_map.68.refs_0_.own_ref, bf16[4,4,4096]{2,1,0:T(4,128)(2,1)S(1)} %collective-permute-done.3.got_ref, ...), custom_call_target="tpu_custom_call" | custom-call | bytes 33554432 | tf_op jit(solution)/shard_map/pallas_call | solution.py:224
  20.9 1.6 %collective-permute-start.4 = (f32[8,2048]{1,0:T(8,128)S(1)}, f32[8,2048]{1,0:T(8,128)S(1)}, u32[]{:S(2)}, u32[]{:S(2)}) collective-permute-start(f32[8,2048]{1,0:T(8,128)S(1)} %get-tuple-element.26), channel_id=1, source_target_pairs={{0,1},{1,0},{2,3},{3,2},{4,5},{5,4},{6,7},{7,6},{8,9},{9,8},{10,11... | collective-permute-start | bytes 196616 | tf_op jit(solution)/shard_map/ppermute | solution.py:211
  22.6 2.6 %collective-permute-start.5 = (f32[8,2048]{1,0:T(8,128)S(1)}, f32[8,2048]{1,0:T(8,128)S(1)}, u32[]{:S(2)}, u32[]{:S(2)}) collective-permute-start(f32[8,2048]{1,0:T(8,128)S(1)} %get-tuple-element.27), channel_id=1, source_target_pairs={{0,2},{1,3},{2,0},{3,1},{4,6},{5,7},{6,4},{7,5},{8,10},{9,11},{10,... | collective-permute-start | bytes 196616 | tf_op jit(solution)/shard_map/ppermute | solution.py:211
  25.2 0.2 collective-permute-start.6
  25.4 0.1 collective-permute-done.4.refs_1_
  25.5 4.1 %collective-permute-done.5.refs_2_ = f32[8,2048]{1,0:T(8,128)S(1)} collective-permute-done((f32[8,2048]{1,0:T(8,128)S(1)}, f32[8,2048]{1,0:T(8,128)S(1)}, u32[]{:S(2)}, u32[]{:S(2)}) %collective-permute-start.5) | collective-permute-done | bytes 65568 | tf_op jit(solution)/shard_map/ppermute | solution.py:211
  29.6 1.7 %collective-permute-done.6.refs_3_ = f32[8,2048]{1,0:T(8,128)S(1)} collective-permute-done((f32[8,2048]{1,0:T(8,128)S(1)}, f32[8,2048]{1,0:T(8,128)S(1)}, u32[]{:S(2)}, u32[]{:S(2)}) %collective-permute-start.6) | collective-permute-done | bytes 65568 | tf_op jit(solution)/shard_map/ppermute | solution.py:211
  31.3 0.7 %shard_map.71 = (f32[8,2048]{1,0:T(8,128)}, f32[8,2048]{1,0:T(8,128)}, f32[8,2048]{1,0:T(8,128)S(1)}) custom-call(f32[8,2048]{1,0:T(8,128)S(1)} %copy-done, f32[8,2048]{1,0:T(8,128)S(1)} %copy-done.1, f32[8,2048]{1,0:T(8,128)S(1)} %get-tuple-element.25.refs_0_, f32[8,2048]{1,0:T(8,128)S(1)} %collective-permute-done.4.refs_1_, ...), custom_call_target="tpu_custom_call" | custom-call | tf_op jit(solution)/shard_map/pallas_call | solution.py:239
  31.9 2.4 %collective-permute-start.9 = (f32[8,2048]{1,0:T(8,128)S(1)}, f32[8,2048]{1,0:T(8,128)S(1)}, u32[]{:S(2)}, u32[]{:S(2)}) collective-permute-start(f32[8,2048]{1,0:T(8,128)S(1)} %get-tuple-element.30.refs_0_), channel_id=1, source_target_pairs={{0,3},{1,2},{2,1},{3,0},{4,7},{5,6},{6,5},{7,4},{8,11},{9,10},{10,... | collective-permute-start | bytes 196616 | tf_op jit(solution)/shard_map/ppermute | solution.py:211
  34.4 0.3 collective-permute-start.8
  34.7 1.6 %collective-permute-start.7 = (f32[8,2048]{1,0:T(8,128)S(1)}, f32[8,2048]{1,0:T(8,128)S(1)}, u32[]{:S(2)}, u32[]{:S(2)}) collective-permute-start(f32[8,2048]{1,0:T(8,128)S(1)} %get-tuple-element.30.refs_0_), channel_id=1, source_target_pairs={{0,1},{1,0},{2,3},{3,2},{4,5},{5,4},{6,7},{7,6},{8,9},{9,8},{10,11... | collective-permute-start | bytes 196616 | tf_op jit(solution)/shard_map/ppermute | solution.py:211
  36.3 2.2 %collective-permute-done.9.refs_3_ = f32[8,2048]{1,0:T(8,128)S(1)} collective-permute-done((f32[8,2048]{1,0:T(8,128)S(1)}, f32[8,2048]{1,0:T(8,128)S(1)}, u32[]{:S(2)}, u32[]{:S(2)}) %collective-permute-start.9) | collective-permute-done | bytes 65568 | tf_op jit(solution)/shard_map/ppermute | solution.py:211
  38.6 2.0 %collective-permute-done.8.refs_2_ = f32[8,2048]{1,0:T(8,128)S(1)} collective-permute-done((f32[8,2048]{1,0:T(8,128)S(1)}, f32[8,2048]{1,0:T(8,128)S(1)}, u32[]{:S(2)}, u32[]{:S(2)}) %collective-permute-start.8) | collective-permute-done | bytes 65568 | tf_op jit(solution)/shard_map/ppermute | solution.py:211
  40.5 10.8 %shard_map.72 = (f32[4,4,4096]{2,1,0:T(4,128)S(1)}, f32[4,4,4096]{2,1,0:T(4,128)S(1)}) custom-call(f32[8,2048]{1,0:T(8,128)S(1)} %get-tuple-element.30.refs_0_, f32[8,2048]{1,0:T(8,128)S(1)} %collective-permute-done.7.refs_1_, f32[8,2048]{1,0:T(8,128)S(1)} %collective-permute-done.8.refs_2_, f32[8,2048]{1,0:T(8,128)S(1)} %collective-permute-done.9.refs_3_, ...), custom_call_target="tpu_custom_call" | custom-call | bytes 33554432 | tf_op jit(solution)/shard_map/pallas_call | solution.py:247
  51.3 0.1 collective-permute-start.10
  51.4 1.5 %collective-permute-done.10.got = f32[4,4,4096]{2,1,0:T(4,128)S(1)} collective-permute-done((f32[4,4,4096]{2,1,0:T(4,128)S(1)}, f32[4,4,4096]{2,1,0:T(4,128)S(1)}, u32[]{:S(2)}, u32[]{:S(2)}) %collective-permute-start.10) | collective-permute-done | bytes 262176 | tf_op jit(solution)/shard_map/ppermute | solution.py:208
  52.9 0.1 shard_map.73
  53.0 1.1 %collective-permute-start.11 = (f32[4,4096]{1,0:T(4,128)S(1)}, f32[4,4096]{1,0:T(4,128)S(1)}, u32[]{:S(2)}, u32[]{:S(2)}) collective-permute-start(f32[4,4096]{1,0:T(4,128)S(1)} %get-tuple-element.34), channel_id=1, source_target_pairs={{0,8},{4,12},{8,0},{12,4},{16,24},{20,28},{24,16},{28,20},{1,9},{5... | collective-permute-start | bytes 196616 | tf_op jit(solution)/shard_map/ppermute | solution.py:208
  54.0 1.5 %collective-permute-start.12 = (f32[4,4096]{1,0:T(4,128)S(1)}, f32[4,4096]{1,0:T(4,128)S(1)}, u32[]{:S(2)}, u32[]{:S(2)}) collective-permute-start(f32[4,4096]{1,0:T(4,128)S(1)} %get-tuple-element.35), channel_id=1, source_target_pairs={{0,16},{4,20},{8,24},{12,28},{16,0},{20,4},{24,8},{28,12},{1,17},{... | collective-permute-start | bytes 196616 | tf_op jit(solution)/shard_map/ppermute | solution.py:208
  55.6 0.9 %collective-permute-start.13 = (f32[4,4096]{1,0:T(4,128)S(1)}, f32[4,4096]{1,0:T(4,128)S(1)}, u32[]{:S(2)}, u32[]{:S(2)}) collective-permute-start(f32[4,4096]{1,0:T(4,128)S(1)} %get-tuple-element.36), channel_id=1, source_target_pairs={{0,24},{4,28},{8,16},{12,20},{16,8},{20,12},{24,0},{28,4},{1,25},{... | collective-permute-start | bytes 196616 | tf_op jit(solution)/shard_map/ppermute | solution.py:208
  56.5 0.8 %collective-permute-done.11 = f32[4,4096]{1,0:T(4,128)S(1)} collective-permute-done((f32[4,4096]{1,0:T(4,128)S(1)}, f32[4,4096]{1,0:T(4,128)S(1)}, u32[]{:S(2)}, u32[]{:S(2)}) %collective-permute-start.11) | collective-permute-done | bytes 65568 | tf_op jit(solution)/shard_map/ppermute | solution.py:208
  57.3 1.0 %collective-permute-done.12 = f32[4,4096]{1,0:T(4,128)S(1)} collective-permute-done((f32[4,4096]{1,0:T(4,128)S(1)}, f32[4,4096]{1,0:T(4,128)S(1)}, u32[]{:S(2)}, u32[]{:S(2)}) %collective-permute-start.12) | collective-permute-done | bytes 65568 | tf_op jit(solution)/shard_map/ppermute | solution.py:208
  58.3 2.4 %collective-permute-done.13 = f32[4,4096]{1,0:T(4,128)S(1)} collective-permute-done((f32[4,4096]{1,0:T(4,128)S(1)}, f32[4,4096]{1,0:T(4,128)S(1)}, u32[]{:S(2)}, u32[]{:S(2)}) %collective-permute-start.13) | collective-permute-done | bytes 65568 | tf_op jit(solution)/shard_map/ppermute | solution.py:208
  60.7 0.7 %add_add_fusion = f32[4,4096]{1,0:T(4,128)} fusion(f32[4,4096]{1,0:T(4,128)S(1)} %collective-permute-done.13, f32[4,4096]{1,0:T(4,128)S(1)} %collective-permute-done.12, f32[4,4096]{1,0:T(4,128)S(1)} %get-tuple-element.33, f32[4,4096]{1,0:T(4,128)S(1)} %collective-permute-done.11), kind=kLoop, calls=%fused_computation | loop fusion | flops 49152 | bytes 327680 | tf_op jit(solution)/shard_map/add | solution.py:270
  (10 shorter events, 0.0 us)
Async XLA Ops:
  0.6 9.6 %copy-start.2 = (bf16[4,4096]{1,0:T(4,128)(2,1)S(1)}, bf16[4,4096]{1,0:T(4,128)(2,1)}, u32[]{:S(2)}) copy-start(bf16[4,4096]{1,0:T(4,128)(2,1)} %refs_1_.2) | copy-start | bytes 98308
  0.6 8.6 %collective-permute-start.1 = (bf16[4,4096]{1,0:T(4,128)(2,1)}, bf16[4,4096]{1,0:T(4,128)(2,1)S(1)}, u32[]{:S(2)}, u32[]{:S(2)}) collective-permute-start(bf16[4,4096]{1,0:T(4,128)(2,1)} %refs_1_.2), channel_id=1, source_target_pairs={{0,16},{4,20},{8,24},{12,28},{16,0},{20,4},{24,8},{28,12},{1,17},{... | collective-permute-start | bytes 98312 | tf_op jit(solution)/shard_map/ppermute | solution.py:208
  3.7 5.6 %collective-permute-start = (bf16[4,4096]{1,0:T(4,128)(2,1)}, bf16[4,4096]{1,0:T(4,128)(2,1)S(1)}, u32[]{:S(2)}, u32[]{:S(2)}) collective-permute-start(bf16[4,4096]{1,0:T(4,128)(2,1)} %refs_1_.2), channel_id=1, source_target_pairs={{0,8},{4,12},{8,0},{12,4},{16,24},{20,28},{24,16},{28,20},{1,9},{5... | collective-permute-start | bytes 98312 | tf_op jit(solution)/shard_map/ppermute | solution.py:208
  5.2 5.0 %collective-permute-start.2 = (bf16[4,4096]{1,0:T(4,128)(2,1)}, bf16[4,4096]{1,0:T(4,128)(2,1)S(1)}, u32[]{:S(2)}, u32[]{:S(2)}) collective-permute-start(bf16[4,4096]{1,0:T(4,128)(2,1)} %refs_1_.2), channel_id=1, source_target_pairs={{0,24},{4,28},{8,16},{12,20},{16,8},{20,12},{24,0},{28,4},{1,25},{... | collective-permute-start | bytes 98312 | tf_op jit(solution)/shard_map/ppermute | solution.py:208
  10.2 2.6 %collective-permute-start.3 = (bf16[4,4,4096]{2,1,0:T(4,128)(2,1)S(1)}, bf16[4,4,4096]{2,1,0:T(4,128)(2,1)S(1)}, u32[]{:S(2)}, u32[]{:S(2)}) collective-permute-start(bf16[4,4,4096]{2,1,0:T(4,128)(2,1)S(1)} %shard_map.68.refs_0_.own_ref), channel_id=1, source_target_pairs={{0,4},{4,0},{8,12},{12,8},{16,20},{20,16},{24,28},{28,24},{1,5},{5... | collective-permute-start | bytes 393224 | tf_op jit(solution)/shard_map/ppermute | solution.py:208
  12.9 18.4 %copy-start = (f32[8,2048]{1,0:T(8,128)S(1)}, f32[8,2048]{1,0:T(8,128)}, u32[]{:S(2)}) copy-start(f32[8,2048]{1,0:T(8,128)} %m_ref.1) | copy-start | bytes 196612
  12.9 18.4 %copy-start.1 = (f32[8,2048]{1,0:T(8,128)S(1)}, f32[8,2048]{1,0:T(8,128)}, u32[]{:S(2)}) copy-start(f32[8,2048]{1,0:T(8,128)} %s_ref.1) | copy-start | bytes 196612
  20.9 4.6 %collective-permute-start.4 = (f32[8,2048]{1,0:T(8,128)S(1)}, f32[8,2048]{1,0:T(8,128)S(1)}, u32[]{:S(2)}, u32[]{:S(2)}) collective-permute-start(f32[8,2048]{1,0:T(8,128)S(1)} %get-tuple-element.26), channel_id=1, source_target_pairs={{0,1},{1,0},{2,3},{3,2},{4,5},{5,4},{6,7},{7,6},{8,9},{9,8},{10,11... | collective-permute-start | bytes 196616 | tf_op jit(solution)/shard_map/ppermute | solution.py:211
  22.6 7.0 %collective-permute-start.5 = (f32[8,2048]{1,0:T(8,128)S(1)}, f32[8,2048]{1,0:T(8,128)S(1)}, u32[]{:S(2)}, u32[]{:S(2)}) collective-permute-start(f32[8,2048]{1,0:T(8,128)S(1)} %get-tuple-element.27), channel_id=1, source_target_pairs={{0,2},{1,3},{2,0},{3,1},{4,6},{5,7},{6,4},{7,5},{8,10},{9,11},{10,... | collective-permute-start | bytes 196616 | tf_op jit(solution)/shard_map/ppermute | solution.py:211
  25.2 6.1 %collective-permute-start.6 = (f32[8,2048]{1,0:T(8,128)S(1)}, f32[8,2048]{1,0:T(8,128)S(1)}, u32[]{:S(2)}, u32[]{:S(2)}) collective-permute-start(f32[8,2048]{1,0:T(8,128)S(1)} %get-tuple-element.28), channel_id=1, source_target_pairs={{0,3},{1,2},{2,1},{3,0},{4,7},{5,6},{6,5},{7,4},{8,11},{9,10},{10,... | collective-permute-start | bytes 196616 | tf_op jit(solution)/shard_map/ppermute | solution.py:211
  31.9 6.6 %collective-permute-start.9 = (f32[8,2048]{1,0:T(8,128)S(1)}, f32[8,2048]{1,0:T(8,128)S(1)}, u32[]{:S(2)}, u32[]{:S(2)}) collective-permute-start(f32[8,2048]{1,0:T(8,128)S(1)} %get-tuple-element.30.refs_0_), channel_id=1, source_target_pairs={{0,3},{1,2},{2,1},{3,0},{4,7},{5,6},{6,5},{7,4},{8,11},{9,10},{10,... | collective-permute-start | bytes 196616 | tf_op jit(solution)/shard_map/ppermute | solution.py:211
  34.4 6.2 %collective-permute-start.8 = (f32[8,2048]{1,0:T(8,128)S(1)}, f32[8,2048]{1,0:T(8,128)S(1)}, u32[]{:S(2)}, u32[]{:S(2)}) collective-permute-start(f32[8,2048]{1,0:T(8,128)S(1)} %get-tuple-element.30.refs_0_), channel_id=1, source_target_pairs={{0,2},{1,3},{2,0},{3,1},{4,6},{5,7},{6,4},{7,5},{8,10},{9,11},{10,... | collective-permute-start | bytes 196616 | tf_op jit(solution)/shard_map/ppermute | solution.py:211
  34.7 5.9 %collective-permute-start.7 = (f32[8,2048]{1,0:T(8,128)S(1)}, f32[8,2048]{1,0:T(8,128)S(1)}, u32[]{:S(2)}, u32[]{:S(2)}) collective-permute-start(f32[8,2048]{1,0:T(8,128)S(1)} %get-tuple-element.30.refs_0_), channel_id=1, source_target_pairs={{0,1},{1,0},{2,3},{3,2},{4,5},{5,4},{6,7},{7,6},{8,9},{9,8},{10,11... | collective-permute-start | bytes 196616 | tf_op jit(solution)/shard_map/ppermute | solution.py:211
  51.3 1.6 %collective-permute-start.10 = (f32[4,4,4096]{2,1,0:T(4,128)S(1)}, f32[4,4,4096]{2,1,0:T(4,128)S(1)}, u32[]{:S(2)}, u32[]{:S(2)}) collective-permute-start(f32[4,4,4096]{2,1,0:T(4,128)S(1)} %get-tuple-element.32), channel_id=1, source_target_pairs={{0,4},{4,0},{8,12},{12,8},{16,20},{20,16},{24,28},{28,24},{1,5},{5... | collective-permute-start | bytes 786440 | tf_op jit(solution)/shard_map/ppermute | solution.py:208
  53.0 4.3 %collective-permute-start.11 = (f32[4,4096]{1,0:T(4,128)S(1)}, f32[4,4096]{1,0:T(4,128)S(1)}, u32[]{:S(2)}, u32[]{:S(2)}) collective-permute-start(f32[4,4096]{1,0:T(4,128)S(1)} %get-tuple-element.34), channel_id=1, source_target_pairs={{0,8},{4,12},{8,0},{12,4},{16,24},{20,28},{24,16},{28,20},{1,9},{5... | collective-permute-start | bytes 196616 | tf_op jit(solution)/shard_map/ppermute | solution.py:208
  54.0 4.3 %collective-permute-start.12 = (f32[4,4096]{1,0:T(4,128)S(1)}, f32[4,4096]{1,0:T(4,128)S(1)}, u32[]{:S(2)}, u32[]{:S(2)}) collective-permute-start(f32[4,4096]{1,0:T(4,128)S(1)} %get-tuple-element.35), channel_id=1, source_target_pairs={{0,16},{4,20},{8,24},{12,28},{16,0},{20,4},{24,8},{28,12},{1,17},{... | collective-permute-start | bytes 196616 | tf_op jit(solution)/shard_map/ppermute | solution.py:208
  55.6 5.2 %collective-permute-start.13 = (f32[4,4096]{1,0:T(4,128)S(1)}, f32[4,4096]{1,0:T(4,128)S(1)}, u32[]{:S(2)}, u32[]{:S(2)}) collective-permute-start(f32[4,4096]{1,0:T(4,128)S(1)} %get-tuple-element.36), channel_id=1, source_target_pairs={{0,24},{4,28},{8,16},{12,20},{16,8},{20,12},{24,0},{28,4},{1,25},{... | collective-permute-start | bytes 196616 | tf_op jit(solution)/shard_map/ppermute | solution.py:208

commit v3 on v0

v3 whole, which is shorter than its diff:
```python
import functools

import jax
import jax.numpy as jnp
from jax import lax
from jax.experimental import pallas as pl
from jax.experimental.pallas import tpu as pltpu
from jax.sharding import PartitionSpec as P

F32, BF16 = jnp.float32, jnp.bfloat16
WHOLE = pl.BlockSpec(memory_space=pltpu.VMEM)
FAR = pl.BlockSpec(memory_space=pltpu.HBM)
ANY = pl.BlockSpec(memory_space=pl.ANY)
TRANSPOSED = (((1,), (1,)), ((), ()))
LIMIT = 6 << 20
PARTS = 4


def f32(*shape):
    return jax.ShapeDtypeStruct(shape, F32)


def turned(rows, width):
    return [pltpu.VMEM((width, rows), BF16)] * 2


def kernel(body, outs, ins, args, scratch=(), moved=0):
    return pl.pallas_call(
        body,
        out_shape=outs,
        in_specs=ins,
        out_specs=jax.tree.map(lambda _: WHOLE, outs),
        scratch_shapes=scratch,
        cost_estimate=pl.CostEstimate(flops=0, bytes_accessed=moved, transcendentals=0) if moved else None,
        compiler_params=pltpu.CompilerParams(vmem_limit_bytes=LIMIT),
    )(*args)


def span(i, size):
    return pl.ds(pl.multiple_of(i * size, size), size)


def adam_moments(moment, second, rotated):
    moment_new = 0.9 * moment + 0.1 * rotated
    second_new = 0.95 * second + 0.05 * rotated * rotated
    normed = moment_new / (1.0 - 0.9**10) / (jnp.sqrt(second_new / (1.0 - 0.95**10)) + 1e-08)
    return (moment_new, second_new, normed)


def split(x):
    high = x.astype(BF16)
    return high, (x - high.astype(F32)).astype(BF16)


def stage_kernel(far, near, sem):
    copy = pltpu.make_async_copy(far, near, sem)
    copy.start()
    copy.wait()


def pack_kernel(own, got, out):
    even = lax.rem(lax.axis_index("rows"), 2) == 0
    own, got = own[...].astype(F32), got[...].astype(F32)
    out[...] = jnp.concatenate([jnp.where(even, own, got), jnp.where(even, got, own)], axis=0).astype(BF16)


def turn(take, high_ref, low_ref, row, rows):
    width = high_ref.shape[0]
    columns = min(width, 512)
    for j in range(width // columns):
        at = slice(j * columns, (j + 1) * columns)
        high, low = split(take(at))
        high_ref[at, pl.ds(row, rows)], low_ref[at, pl.ds(row, rows)] = high.T, low.T


def load_kernel(_, b_ref, near, sems):
    count = sems.shape[0]
    rows = near.shape[0] // count
    copies = [
        pltpu.make_async_copy(b_ref.at[pl.ds(i * rows, rows), :], near.at[pl.ds(i * rows, rows), :], sems.at[i])
        for i in range(count)
    ]
    for copy in copies:
        copy.start()
    for copy in copies:
        copy.wait()


def turn_kernel(b_ref, *refs):
    high_ref, low_ref = refs[-2:]
    rows = min(b_ref.shape[0], 512)
    for i in range(b_ref.shape[0] // rows):
        turn(lambda at, i=i: b_ref[i * rows : (i + 1) * rows, at], high_ref, low_ref, i * rows, rows)


def rotate_kernel(n, chips, *refs):
    blocks, (ready, b_ref), refs = refs[:chips], refs[chips : chips + 2], refs[chips + 2 :]
    outs, parts, (g_ref, total, sems) = refs[:n], refs[n : n + PARTS - 1], refs[n + PARTS - 1 :]
    part, width = parts[0].shape
    rows, columns = min(part, 256), min(width, 256)
    tiles = [(p, i) for p in range(PARTS - 1) for i in range(part // rows)]

    def copy(k):
        p, i = tiles[k]
        return pltpu.make_async_copy(
            b_ref.at[pl.ds((p + 1) * part + i * rows, rows), :], parts[p].at[pl.ds(i * rows, rows), :], sems.at[k]
        )

    def copy_at(p, i):
        return pltpu.make_async_copy(
            b_ref.at[span((p + 1) * (part // rows) + i, rows), :],
            parts[p].at[span(i, rows), :],
            sems.at[p * (part // rows) + i],
        )

    for k in range(len(tiles)):
        copy(k).start()
    g_ref[...] = jnp.concatenate([block[...].astype(F32) for block in blocks], axis=0).astype(BF16)
    total[...] = jnp.zeros_like(total)
    for p, ref in enumerate((ready, *parts)):

        def tile(i, _, p=p, ref=ref):
            if p:
                copy_at(p - 1, i).wait()
            g = g_ref[:, pl.ds(pl.multiple_of(p * part + i * rows, rows), rows)]
            for j in range(width // columns):
                at = slice(j * columns, (j + 1) * columns)
                high, low = split(ref[span(i, rows), at])
                total[:, at] += jnp.dot(g, high, preferred_element_type=F32) + jnp.dot(
                    g, low, preferred_element_type=F32
                )
            return 0

        lax.fori_loop(0, part // rows, tile, 0)
    pair = blocks[0].shape[0]
    chip = lax.axis_index("rows") // 2
    each = chips // n
    for s, out in enumerate(outs):
        place = (lax.axis_index("cols") ^ s) * each
        for i in range(each):
            out[i * pair : (i + 1) * pair, :] = total[span(chip ^ (place + i), pair), :]


def normed_kernel(n, m_ref, s_ref, *refs):
    parts, (normed, rotated) = refs[:n], refs[-2:]
    total = parts[0][...]
    for part in parts[1:]:
        total = total + part[...]
    rotated[...] = total
    normed[...] = adam_moments(m_ref[...], s_ref[...], total)[2]


def moments_kernel(m_ref, s_ref, rotated, moment_new, second_new):
    moment_new[...], second_new[...], _ = adam_moments(m_ref[...], s_ref[...], rotated[...])


def back_kernel(n, kept, *refs):
    blocks, pieces, rest = refs[:n], refs[n : n + kept], refs[n + kept : -5]
    keep, send, x_ref, x2_ref, o_ref = refs[-5:]
    each, rows = blocks[0].shape[0], x_ref.shape[0]
    for s, block in enumerate(blocks):
        x_ref[span(lax.axis_index("cols") ^ s, each), :] = block[...]
    high, low = split(x_ref[...])
    x2_ref[:rows, :], x2_ref[rows:, :] = high, low
    part = rest[0].shape[0]
    size = min(part, 512)

    def store(to, first, second):
        o_ref[:, to : to + size] = first[:rows] + first[rows:] + second

    for p, (high, low) in enumerate(zip(pieces[::2], pieces[1::2])):
        for i in range(part // size):
            at = slice(i * size, (i + 1) * size)
            first = jnp.dot(x2_ref[...], high[:, at], preferred_element_type=F32)
            second = jnp.dot(x2_ref[:rows, :], low[:, at], preferred_element_type=F32)
            store(p * part + i * size, first, second)
    for p, ref in enumerate(rest):
        for i in range(part // size):
            high, low = split(ref[i * size : (i + 1) * size, :])
            first = lax.dot_general(x2_ref[...], high, TRANSPOSED, preferred_element_type=F32)
            second = lax.dot_general(x2_ref[:rows, :], low, TRANSPOSED, preferred_element_type=F32)
            store((len(pieces) // 2 + p) * part + i * size, first, second)
    odd = lax.rem(lax.axis_index("rows"), 2) == 1
    chips, four, height = keep.shape
    whole = o_ref[...].reshape(chips, 2, four, height)
    keep[...] = jnp.where(odd, whole[:, 1], whole[:, 0])
    send[...] = jnp.where(odd, whole[:, 0], whole[:, 1])


def fold_kernel(keep, got, *outs):
    chip = lax.axis_index("rows") // 2
    total = keep[...] + got[...]
    for s, out in enumerate(outs):
        block = total[0]
        for i in range(1, len(outs)):
            block = jnp.where((chip ^ s) == i, total[i], block)
        out[...] = block


def step_on_device(gradient, basis, moment, second):
    n, m = lax.axis_size("cols"), lax.axis_size("rows")
    chips = m // 2
    each, width = moment.shape
    four, height = gradient.shape
    part = height // PARTS
    partbytes = part * width * 4

    def along(x, axis, size, s):
        return lax.ppermute(x, axis, [(i, i ^ s) for i in range(size)])

    def along_rows(x, s):
        return along(x, "rows", m, s)

    def along_cols(x, s):
        return along(x, "cols", n, s)

    basis = pltpu.with_memory_space_constraint(basis, pltpu.HBM)
    partner = along_rows(gradient, 1)
    own = kernel(
        stage_kernel,
        pltpu.VMEM(gradient.shape, BF16),
        [FAR],
        (pltpu.with_memory_space_constraint(gradient, pltpu.HBM),),
        [pltpu.SemaphoreType.DMA],
        four * height * 4,
    )
    own = kernel(pack_kernel, jax.ShapeDtypeStruct((2 * four, height), BF16), [WHOLE] * 2, (own, partner))
    from_chips = [own] + [along_rows(own, 2 * s) for s in range(1, chips)]
    first = kernel(
        load_kernel,
        pltpu.VMEM((part, width), F32),
        [ANY, FAR],
        (own, basis),
        [pltpu.SemaphoreType.DMA((4,))],
        2 * partbytes,
    )
    results = kernel(
        functools.partial(rotate_kernel, n, chips),
        [f32(each, width)] * n + [pltpu.VMEM((part, width), F32)] * (PARTS - 1),
        [WHOLE] * (chips + 1) + [FAR],
        (*from_chips, first, basis),
        [
            pltpu.VMEM((n * each, height), BF16),
            pltpu.VMEM((n * each, width), F32),
            pltpu.SemaphoreType.DMA((height // min(part, 256),)),
        ],
        PARTS * partbytes,
    )
    parts, (early, later, *rest) = results[:n], [
        pltpu.with_memory_space_constraint(x, pltpu.VMEM) for x in (first, *results[n:])
    ]
    parts = [parts[0]] + [along_cols(parts[s], s) for s in range(1, n)]
    pieces = list(
        kernel(turn_kernel, turned(part, width), [WHOLE] * (2 + len(rest)), (early, later, *rest), (), 2 * partbytes)
    )
    pieces = [pltpu.with_memory_space_constraint(x, pltpu.VMEM) for x in pieces]
    normed, rotated = kernel(
        functools.partial(normed_kernel, n),
        [f32(each, width)] * 2,
        [WHOLE] * (n + 3 + len(pieces) + len(rest)),
        (moment, second, *parts, *pieces, later, *rest),
    )
    moment_new, second_new = kernel(
        moments_kernel, [f32(each, width)] * 2, [WHOLE] * 3, (moment, second, rotated), (), 8 * each * width * 4
    )
    blocks = [normed] + [along_cols(normed, s) for s in range(1, n)]
    pieces += list(kernel(turn_kernel, turned(part, width), [WHOLE] * (1 + len(rest)), (later, *rest), (), 2 * partbytes))
    keep, send = kernel(
        functools.partial(back_kernel, n, len(pieces)),
        [f32(chips, four, height)] * 2,
        [WHOLE] * (n + len(pieces) + len(rest)),
        (*blocks, *pieces, *rest),
        [
            pltpu.VMEM((n * each, width), F32),
            pltpu.VMEM((2 * n * each, width), BF16),
            pltpu.VMEM((n * each, height), F32),
        ],
        PARTS * partbytes,
    )
    got = along_rows(send, 1)
    halves = kernel(fold_kernel, [f32(four, height)] * chips, [WHOLE] * 2, (keep, got))
    update = halves[0]
    for s in range(1, chips):
        update = update + along_rows(halves[s], 2 * s)
    return (update, moment_new, second_new)


def solution(mesh):
    placed = (P("rows", "cols"), P("cols", "rows"), P("cols", "rows"), P("cols", "rows"))
    return jax.shard_map(
        step_on_device,
        mesh=mesh,
        in_specs=placed,
        out_specs=(P("rows", "cols"), P("cols", "rows"), P("cols", "rows")),
        check_vma=False,
    )
```

time: 168 us -> 56.3 us (0.34)
  waiting for transfers between devices: 72.7 us -> 10.2 us
  matrix products: 51.3 us -> 0 us
  Pallas kernels: 0 us -> 26.9 us
  blocking collectives: 24.9 us -> 0 us
  starting transfers between devices: 0.08 us -> 17.6 us
  between operations: 14.7 us -> 0.74 us
  local copies, waits for them, and re-layouts: 2.21 us -> 0.01 us
    unnamed x3 -> x0, waiting for transfers between devices: 52.3 us -> none
    dot_general x2 -> x0, matrix products: 51.3 us -> none  [the longest x1 34.3 us: body(): lax.dot_general(normed_all, basis, (((1,), (1,)), ((), ())), precision=la...]
    pallas_call x0 -> x10, Pallas kernels: none -> 26.9 us  [kernel(): pl.pallas_call(body, out_shape=outs, in_specs=ins, out_specs=jax.tree.map...]
    all_gather x2 -> x0, blocking collectives: 24.9 us -> none  [the longest x1 13.9 us: body(): normed_all = lax.all_gather(normed, 'cols', axis=0, tiled=True)]
    reduce_scatter x1 -> x0, waiting for transfers between devices: 20.4 us -> none  [body(): lax.psum_scatter(partial_value, 'cols', scatter_dimension=0, tiled=True)]
    ppermute x0 -> x14, starting transfers between devices: none -> 17.6 us  [along(): return lax.ppermute(x, axis, [(i, i ^ s) for i in range(size)])]
    ppermute x0 -> x14, waiting for transfers between devices: none -> 10.2 us  [along(): return lax.ppermute(x, axis, [(i, i ^ s) for i in range(size)])]
    unnamed x9 -> x4, local copies, waits for them, and re-layouts: 2.21 us -> 0.01 us
  transfers between devices with their start and end apart: 2 -> 14, of which waited for: 2 -> 10; matrix products, arithmetic and copies ran while one was open for 0% -> 0% of each run, Pallas kernels for 0% -> 18%
where the time goes in v3:
time: 56.3 us; the launch traced here: 56.1 us
  Pallas kernels  26.9 us (48%)
  starting transfers between devices  17.6 us (31%)
  waiting for transfers between devices  10.2 us (18%)
  between operations  0.74 us (1%)
  other arithmetic  0.67 us (1%)
    pallas_call x10, Pallas kernels, kernel(): pl.pallas_call(body, out_shape=outs, in_specs=ins, out_specs=jax.tree.map...  26.9 us
    ppermute x14, starting transfers between devices, along(): return lax.ppermute(x, axis, [(i, i ^ s) for i in range(size)])  17.6 us
    ppermute x14, waiting for transfers between devices, along(): return lax.ppermute(x, axis, [(i, i ^ s) for i in range(size)])  10.2 us
  transfers between devices with their start and end apart: 14, of which 10 were waited for; matrix products, arithmetic and copies ran while one was open for 0% of the time, Pallas kernels for 18%

profile of v3, /device:TPU:0, one launch (start us, length us, event | category | flops | bytes accessed | tf_op | source)
XLA Modules:
  0.0 56.1 jit_solution(168857122709779320)
XLA Ops:
  0.6 0.6 collective-permute-start
  1.2 0.8 %shard_map.67.own = bf16[4,4096]{1,0:T(4,128)(2,1)S(1)} custom-call(bf16[4,4096]{1,0:T(4,128)(2,1)} %far.1), custom_call_target="tpu_custom_call" | custom-call | bytes 65536 | tf_op jit(solution)/shard_map/pallas_call | solution.py:28
  2.0 0.3 collective-permute-done.got
  2.3 3.8 %collective-permute-start.3 = (bf16[8,4096]{1,0:T(8,128)(2,1)S(1)}, bf16[8,4096]{1,0:T(8,128)(2,1)S(1)}, u32[]{:S(2)}, u32[]{:S(2)}) collective-permute-start(bf16[8,4096]{1,0:T(8,128)(2,1)S(1)} %shard_map.68._.refs_0_), channel_id=1, source_target_pairs={{0,24},{4,28},{8,16},{12,20},{16,8},{20,12},{24,0},{28,4},{1,25},{... | collective-permute-start | bytes 196616 | tf_op jit(solution)/shard_map/ppermute | solution.py:209
  6.1 0.5 collective-permute-start.2
  6.6 0.1 collective-permute-start.1
  6.8 3.5 %shard_map.69.refs_4_.b_ref = f32[1024,2048]{1,0:T(8,128)S(1)} custom-call(bf16[8,4096]{1,0:T(8,128)(2,1)S(1)} %shard_map.68._.refs_0_, f32[4096,2048]{1,0:T(8,128)} %refs_5_.1), custom_call_target="tpu_custom_call" | custom-call | bytes 16777216 | tf_op jit(solution)/shard_map/pallas_call | solution.py:28
  10.3 0.1 collective-permute-done.2.refs_2_
  10.4 0.5 collective-permute-done.1.refs_1_
  10.9 8.9 %shard_map.70 = (f32[8,2048]{1,0:T(8,128)S(1)}, f32[8,2048]{1,0:T(8,128)S(1)}, f32[8,2048]{1,0:T(8,128)S(1)}, f32[8,2048]{1,0:T(8,128)S(1)}, f32[1024,2048]{1,0:...) custom-call(bf16[8,4096]{1,0:T(8,128)(2,1)S(1)} %shard_map.68._.refs_0_, ...), custom_call_target="tpu_custom_call" | custom-call | bytes 33554432 | tf_op jit(solution)/shard_map/pallas_call | solution.py:28
  19.8 1.6 %collective-permute-start.4 = (f32[8,2048]{1,0:T(8,128)S(1)}, f32[8,2048]{1,0:T(8,128)S(1)}, u32[]{:S(2)}, u32[]{:S(2)}) collective-permute-start(f32[8,2048]{1,0:T(8,128)S(1)} %get-tuple-element.25), channel_id=1, source_target_pairs={{0,1},{1,0},{2,3},{3,2},{4,5},{5,4},{6,7},{7,6},{8,9},{9,8},{10,11... | collective-permute-start | bytes 196616 | tf_op jit(solution)/shard_map/ppermute | solution.py:209
  21.5 2.6 %collective-permute-start.5 = (f32[8,2048]{1,0:T(8,128)S(1)}, f32[8,2048]{1,0:T(8,128)S(1)}, u32[]{:S(2)}, u32[]{:S(2)}) collective-permute-start(f32[8,2048]{1,0:T(8,128)S(1)} %get-tuple-element.26), channel_id=1, source_target_pairs={{0,2},{1,3},{2,0},{3,1},{4,6},{5,7},{6,4},{7,5},{8,10},{9,11},{10,... | collective-permute-start | bytes 196616 | tf_op jit(solution)/shard_map/ppermute | solution.py:209
  24.0 0.2 collective-permute-start.6
  24.3 2.5 %shard_map.71 = (bf16[2048,1024]{1,0:T(8,128)(2,1)S(1)}, bf16[2048,1024]{1,0:T(8,128)(2,1)S(1)}) custom-call(f32[1024,2048]{1,0:T(8,128)S(1)} %shard_map.69.refs_4_.b_ref, f32[1024,2048]{1,0:T(8,128)S(1)} %get-tuple-element.28.refs_0_.refs_6_.b_ref, f32[1024,2048]{1,0:T(8,128)S(1)} %get-tuple-element.29.refs_1_.refs_7_.refs_0_.refs_8_, ...), custom_call_target="tpu_custom_call" | custom-call | bytes 16777216 | tf_op jit(solution)/shard_map/pallas_call | solution.py:28
  26.8 1.3 %collective-permute-done.5.refs_2_ = f32[8,2048]{1,0:T(8,128)S(1)} collective-permute-done((f32[8,2048]{1,0:T(8,128)S(1)}, f32[8,2048]{1,0:T(8,128)S(1)}, u32[]{:S(2)}, u32[]{:S(2)}) %collective-permute-start.5) | collective-permute-done | bytes 65568 | tf_op jit(solution)/shard_map/ppermute | solution.py:209
  28.0 2.2 %collective-permute-done.6.refs_3_ = f32[8,2048]{1,0:T(8,128)S(1)} collective-permute-done((f32[8,2048]{1,0:T(8,128)S(1)}, f32[8,2048]{1,0:T(8,128)S(1)}, u32[]{:S(2)}, u32[]{:S(2)}) %collective-permute-start.6) | collective-permute-done | bytes 65568 | tf_op jit(solution)/shard_map/ppermute | solution.py:209
  30.3 1.1 %collective-permute-start.9 = (f32[8,2048]{1,0:T(8,128)S(1)}, f32[8,2048]{1,0:T(8,128)S(1)}, u32[]{:S(2)}, u32[]{:S(2)}) collective-permute-start(f32[8,2048]{1,0:T(8,128)S(1)} %get-tuple-element.33.refs_0_), channel_id=1, source_target_pairs={{0,3},{1,2},{2,1},{3,0},{4,7},{5,6},{6,5},{7,4},{8,11},{9,10},{10,... | collective-permute-start | bytes 196616 | tf_op jit(solution)/shard_map/ppermute | solution.py:209
  31.3 0.1 collective-permute-start.8
  31.4 3.3 %collective-permute-start.7 = (f32[8,2048]{1,0:T(8,128)S(1)}, f32[8,2048]{1,0:T(8,128)S(1)}, u32[]{:S(2)}, u32[]{:S(2)}) collective-permute-start(f32[8,2048]{1,0:T(8,128)S(1)} %get-tuple-element.33.refs_0_), channel_id=1, source_target_pairs={{0,1},{1,0},{2,3},{3,2},{4,5},{5,4},{6,7},{7,6},{8,9},{9,8},{10,11... | collective-permute-start | bytes 196616 | tf_op jit(solution)/shard_map/ppermute | solution.py:209
  34.7 2.5 %shard_map.73 = (bf16[2048,1024]{1,0:T(8,128)(2,1)S(1)}, bf16[2048,1024]{1,0:T(8,128)(2,1)S(1)}) custom-call(f32[1024,2048]{1,0:T(8,128)S(1)} %get-tuple-element.28.refs_0_.refs_6_.b_ref, f32[1024,2048]{1,0:T(8,128)S(1)} %get-tuple-element.29.refs_1_.refs_7_.refs_0_.refs_8_, f32[1024,2048]{1,0:T(8,128)S(1)} %get-tuple-element.30.refs_2_.refs_8_.refs_1_.refs_9_), custom_call_target="tpu_custom_call" | custom-call | bytes 16777216 | tf_op jit(solution)/shard_map/pallas_call | solution.py:28
  37.2 0.6 %collective-permute-done.8.refs_2_ = f32[8,2048]{1,0:T(8,128)S(1)} collective-permute-done((f32[8,2048]{1,0:T(8,128)S(1)}, f32[8,2048]{1,0:T(8,128)S(1)}, u32[]{:S(2)}, u32[]{:S(2)}) %collective-permute-start.8) | collective-permute-done | bytes 65568 | tf_op jit(solution)/shard_map/ppermute | solution.py:209
  37.8 8.0 %shard_map.74 = (f32[4,4,4096]{2,1,0:T(4,128)S(1)}, f32[4,4,4096]{2,1,0:T(4,128)S(1)}) custom-call(f32[8,2048]{1,0:T(8,128)S(1)} %get-tuple-element.33.refs_0_, f32[8,2048]{1,0:T(8,128)S(1)} %collective-permute-done.7.refs_1_, f32[8,2048]{1,0:T(8,128)S(1)} %collective-permute-done.8.refs_2_, f32[8,2048]{1,0:T(8,128)S(1)} %collective-permute-done.9.refs_3_, ...), custom_call_target="tpu_custom_call" | custom-call | bytes 33554432 | tf_op jit(solution)/shard_map/pallas_call | solution.py:28
  45.8 0.1 collective-permute-start.10
  45.9 1.5 %collective-permute-done.10.got = f32[4,4,4096]{2,1,0:T(4,128)S(1)} collective-permute-done((f32[4,4,4096]{2,1,0:T(4,128)S(1)}, f32[4,4,4096]{2,1,0:T(4,128)S(1)}, u32[]{:S(2)}, u32[]{:S(2)}) %collective-permute-start.10) | collective-permute-done | bytes 262176 | tf_op jit(solution)/shard_map/ppermute | solution.py:209
  47.5 1.3 %collective-permute-start.11 = (f32[4,4096]{1,0:T(4,128)S(1)}, f32[4,4096]{1,0:T(4,128)S(1)}, u32[]{:S(2)}, u32[]{:S(2)}) collective-permute-start(f32[4,4096]{1,0:T(4,128)S(1)} %get-tuple-element.39), channel_id=1, source_target_pairs={{0,8},{4,12},{8,0},{12,4},{16,24},{20,28},{24,16},{28,20},{1,9},{5... | collective-permute-start | bytes 196616 | tf_op jit(solution)/shard_map/ppermute | solution.py:209
  48.8 1.5 %collective-permute-start.12 = (f32[4,4096]{1,0:T(4,128)S(1)}, f32[4,4096]{1,0:T(4,128)S(1)}, u32[]{:S(2)}, u32[]{:S(2)}) collective-permute-start(f32[4,4096]{1,0:T(4,128)S(1)} %get-tuple-element.40), channel_id=1, source_target_pairs={{0,16},{4,20},{8,24},{12,28},{16,0},{20,4},{24,8},{28,12},{1,17},{... | collective-permute-start | bytes 196616 | tf_op jit(solution)/shard_map/ppermute | solution.py:209
  50.3 0.8 %collective-permute-start.13 = (f32[4,4096]{1,0:T(4,128)S(1)}, f32[4,4096]{1,0:T(4,128)S(1)}, u32[]{:S(2)}, u32[]{:S(2)}) collective-permute-start(f32[4,4096]{1,0:T(4,128)S(1)} %get-tuple-element.41), channel_id=1, source_target_pairs={{0,24},{4,28},{8,16},{12,20},{16,8},{20,12},{24,0},{28,4},{1,25},{... | collective-permute-start | bytes 196616 | tf_op jit(solution)/shard_map/ppermute | solution.py:209
  51.0 0.7 %shard_map.76 = (f32[8,2048]{1,0:T(8,128)}, f32[8,2048]{1,0:T(8,128)}) custom-call(f32[8,2048]{1,0:T(8,128)S(1)} %copy-done, f32[8,2048]{1,0:T(8,128)S(1)} %copy-done.1, f32[8,2048]{1,0:T(8,128)S(1)} %get-tuple-element.42.rotated), custom_call_target="tpu_custom_call" | custom-call | bytes 524288 | tf_op jit(solution)/shard_map/pallas_call | solution.py:28
  51.7 0.1 collective-permute-done.11
  51.8 1.2 %collective-permute-done.12 = f32[4,4096]{1,0:T(4,128)S(1)} collective-permute-done((f32[4,4096]{1,0:T(4,128)S(1)}, f32[4,4096]{1,0:T(4,128)S(1)}, u32[]{:S(2)}, u32[]{:S(2)}) %collective-permute-start.12) | collective-permute-done | bytes 65568 | tf_op jit(solution)/shard_map/ppermute | solution.py:209
  53.0 2.4 %collective-permute-done.13 = f32[4,4096]{1,0:T(4,128)S(1)} collective-permute-done((f32[4,4096]{1,0:T(4,128)S(1)}, f32[4,4096]{1,0:T(4,128)S(1)}, u32[]{:S(2)}, u32[]{:S(2)}) %collective-permute-start.13) | collective-permute-done | bytes 65568 | tf_op jit(solution)/shard_map/ppermute | solution.py:209
  55.4 0.7 %add_add_fusion = f32[4,4096]{1,0:T(4,128)} fusion(f32[4,4096]{1,0:T(4,128)S(1)} %collective-permute-done.13, f32[4,4096]{1,0:T(4,128)S(1)} %collective-permute-done.12, f32[4,4096]{1,0:T(4,128)S(1)} %get-tuple-element.38, f32[4,4096]{1,0:T(4,128)S(1)} %collective-permute-done.11), kind=kLoop, calls=%fused_computation | loop fusion | flops 49152 | bytes 327680 | tf_op jit(solution)/shard_map/add | solution.py:284
  (11 shorter events, 0.2 us)
Async XLA Ops:
  0.6 1.6 %collective-permute-start = (bf16[4,4096]{1,0:T(4,128)(2,1)}, bf16[4,4096]{1,0:T(4,128)(2,1)S(1)}, u32[]{:S(2)}, u32[]{:S(2)}) collective-permute-start(bf16[4,4096]{1,0:T(4,128)(2,1)} %far.1), channel_id=1, source_target_pairs={{0,4},{4,0},{8,12},{12,8},{16,20},{20,16},{24,28},{28,24},{1,5},{5... | collective-permute-start | bytes 98312 | tf_op jit(solution)/shard_map/ppermute | solution.py:209
  2.3 8.0 %collective-permute-start.3 = (bf16[8,4096]{1,0:T(8,128)(2,1)S(1)}, bf16[8,4096]{1,0:T(8,128)(2,1)S(1)}, u32[]{:S(2)}, u32[]{:S(2)}) collective-permute-start(bf16[8,4096]{1,0:T(8,128)(2,1)S(1)} %shard_map.68._.refs_0_), channel_id=1, source_target_pairs={{0,24},{4,28},{8,16},{12,20},{16,8},{20,12},{24,0},{28,4},{1,25},{... | collective-permute-start | bytes 196616 | tf_op jit(solution)/shard_map/ppermute | solution.py:209
  6.1 4.3 %collective-permute-start.2 = (bf16[8,4096]{1,0:T(8,128)(2,1)S(1)}, bf16[8,4096]{1,0:T(8,128)(2,1)S(1)}, u32[]{:S(2)}, u32[]{:S(2)}) collective-permute-start(bf16[8,4096]{1,0:T(8,128)(2,1)S(1)} %shard_map.68._.refs_0_), channel_id=1, source_target_pairs={{0,16},{4,20},{8,24},{12,28},{16,0},{20,4},{24,8},{28,12},{1,17},{... | collective-permute-start | bytes 196616 | tf_op jit(solution)/shard_map/ppermute | solution.py:209
  6.6 4.3 %collective-permute-start.1 = (bf16[8,4096]{1,0:T(8,128)(2,1)S(1)}, bf16[8,4096]{1,0:T(8,128)(2,1)S(1)}, u32[]{:S(2)}, u32[]{:S(2)}) collective-permute-start(bf16[8,4096]{1,0:T(8,128)(2,1)S(1)} %shard_map.68._.refs_0_), channel_id=1, source_target_pairs={{0,8},{4,12},{8,0},{12,4},{16,24},{20,28},{24,16},{28,20},{1,9},{5... | collective-permute-start | bytes 196616 | tf_op jit(solution)/shard_map/ppermute | solution.py:209
  19.8 6.9 %collective-permute-start.4 = (f32[8,2048]{1,0:T(8,128)S(1)}, f32[8,2048]{1,0:T(8,128)S(1)}, u32[]{:S(2)}, u32[]{:S(2)}) collective-permute-start(f32[8,2048]{1,0:T(8,128)S(1)} %get-tuple-element.25), channel_id=1, source_target_pairs={{0,1},{1,0},{2,3},{3,2},{4,5},{5,4},{6,7},{7,6},{8,9},{9,8},{10,11... | collective-permute-start | bytes 196616 | tf_op jit(solution)/shard_map/ppermute | solution.py:209
  21.5 6.6 %collective-permute-start.5 = (f32[8,2048]{1,0:T(8,128)S(1)}, f32[8,2048]{1,0:T(8,128)S(1)}, u32[]{:S(2)}, u32[]{:S(2)}) collective-permute-start(f32[8,2048]{1,0:T(8,128)S(1)} %get-tuple-element.26), channel_id=1, source_target_pairs={{0,2},{1,3},{2,0},{3,1},{4,6},{5,7},{6,4},{7,5},{8,10},{9,11},{10,... | collective-permute-start | bytes 196616 | tf_op jit(solution)/shard_map/ppermute | solution.py:209
  24.0 6.2 %collective-permute-start.6 = (f32[8,2048]{1,0:T(8,128)S(1)}, f32[8,2048]{1,0:T(8,128)S(1)}, u32[]{:S(2)}, u32[]{:S(2)}) collective-permute-start(f32[8,2048]{1,0:T(8,128)S(1)} %get-tuple-element.27), channel_id=1, source_target_pairs={{0,3},{1,2},{2,1},{3,0},{4,7},{5,6},{6,5},{7,4},{8,11},{9,10},{10,... | collective-permute-start | bytes 196616 | tf_op jit(solution)/shard_map/ppermute | solution.py:209
  24.3 5.9 %copy-start = (f32[8,2048]{1,0:T(8,128)S(1)}, f32[8,2048]{1,0:T(8,128)}, u32[]{:S(2)}) copy-start(f32[8,2048]{1,0:T(8,128)} %m_ref.3) | copy-start | bytes 196612
  24.3 5.9 %copy-start.1 = (f32[8,2048]{1,0:T(8,128)S(1)}, f32[8,2048]{1,0:T(8,128)}, u32[]{:S(2)}) copy-start(f32[8,2048]{1,0:T(8,128)} %s_ref.3) | copy-start | bytes 196612
  30.3 6.9 %collective-permute-start.9 = (f32[8,2048]{1,0:T(8,128)S(1)}, f32[8,2048]{1,0:T(8,128)S(1)}, u32[]{:S(2)}, u32[]{:S(2)}) collective-permute-start(f32[8,2048]{1,0:T(8,128)S(1)} %get-tuple-element.33.refs_0_), channel_id=1, source_target_pairs={{0,3},{1,2},{2,1},{3,0},{4,7},{5,6},{6,5},{7,4},{8,11},{9,10},{10,... | collective-permute-start | bytes 196616 | tf_op jit(solution)/shard_map/ppermute | solution.py:209
  31.3 6.5 %collective-permute-start.8 = (f32[8,2048]{1,0:T(8,128)S(1)}, f32[8,2048]{1,0:T(8,128)S(1)}, u32[]{:S(2)}, u32[]{:S(2)}) collective-permute-start(f32[8,2048]{1,0:T(8,128)S(1)} %get-tuple-element.33.refs_0_), channel_id=1, source_target_pairs={{0,2},{1,3},{2,0},{3,1},{4,6},{5,7},{6,4},{7,5},{8,10},{9,11},{10,... | collective-permute-start | bytes 196616 | tf_op jit(solution)/shard_map/ppermute | solution.py:209
  31.4 6.4 %collective-permute-start.7 = (f32[8,2048]{1,0:T(8,128)S(1)}, f32[8,2048]{1,0:T(8,128)S(1)}, u32[]{:S(2)}, u32[]{:S(2)}) collective-permute-start(f32[8,2048]{1,0:T(8,128)S(1)} %get-tuple-element.33.refs_0_), channel_id=1, source_target_pairs={{0,1},{1,0},{2,3},{3,2},{4,5},{5,4},{6,7},{7,6},{8,9},{9,8},{10,11... | collective-permute-start | bytes 196616 | tf_op jit(solution)/shard_map/ppermute | solution.py:209
  45.8 1.6 %collective-permute-start.10 = (f32[4,4,4096]{2,1,0:T(4,128)S(1)}, f32[4,4,4096]{2,1,0:T(4,128)S(1)}, u32[]{:S(2)}, u32[]{:S(2)}) collective-permute-start(f32[4,4,4096]{2,1,0:T(4,128)S(1)} %get-tuple-element.37), channel_id=1, source_target_pairs={{0,4},{4,0},{8,12},{12,8},{16,20},{20,16},{24,28},{28,24},{1,5},{5... | collective-permute-start | bytes 786440 | tf_op jit(solution)/shard_map/ppermute | solution.py:209
  47.5 4.3 %collective-permute-start.11 = (f32[4,4096]{1,0:T(4,128)S(1)}, f32[4,4096]{1,0:T(4,128)S(1)}, u32[]{:S(2)}, u32[]{:S(2)}) collective-permute-start(f32[4,4096]{1,0:T(4,128)S(1)} %get-tuple-element.39), channel_id=1, source_target_pairs={{0,8},{4,12},{8,0},{12,4},{16,24},{20,28},{24,16},{28,20},{1,9},{5... | collective-permute-start | bytes 196616 | tf_op jit(solution)/shard_map/ppermute | solution.py:209
  48.8 4.3 %collective-permute-start.12 = (f32[4,4096]{1,0:T(4,128)S(1)}, f32[4,4096]{1,0:T(4,128)S(1)}, u32[]{:S(2)}, u32[]{:S(2)}) collective-permute-start(f32[4,4096]{1,0:T(4,128)S(1)} %get-tuple-element.40), channel_id=1, source_target_pairs={{0,16},{4,20},{8,24},{12,28},{16,0},{20,4},{24,8},{28,12},{1,17},{... | collective-permute-start | bytes 196616 | tf_op jit(solution)/shard_map/ppermute | solution.py:209
  50.3 5.2 %collective-permute-start.13 = (f32[4,4096]{1,0:T(4,128)S(1)}, f32[4,4096]{1,0:T(4,128)S(1)}, u32[]{:S(2)}, u32[]{:S(2)}) collective-permute-start(f32[4,4096]{1,0:T(4,128)S(1)} %get-tuple-element.41), channel_id=1, source_target_pairs={{0,24},{4,28},{8,16},{12,20},{16,8},{20,12},{24,0},{28,4},{1,25},{... | collective-permute-start | bytes 196616 | tf_op jit(solution)/shard_map/ppermute | solution.py:209

commit v4 on v3

--- a/solution.py
+++ b/solution.py
@@ -13,7 +13,7 @@
 ANY = pl.BlockSpec(memory_space=pl.ANY)
 TRANSPOSED = (((1,), (1,)), ((), ()))
 LIMIT = 6 << 20
-PARTS = 4
+PARTS = (5, 5, 3, 3)
 
 
 def f32(*shape):
@@ -88,41 +88,33 @@
 
 def turn_kernel(b_ref, *refs):
     high_ref, low_ref = refs[-2:]
-    rows = min(b_ref.shape[0], 512)
+    rows = min(b_ref.shape[0], 256)
     for i in range(b_ref.shape[0] // rows):
         turn(lambda at, i=i: b_ref[i * rows : (i + 1) * rows, at], high_ref, low_ref, i * rows, rows)
 
 
 def rotate_kernel(n, chips, *refs):
     blocks, (ready, b_ref), refs = refs[:chips], refs[chips : chips + 2], refs[chips + 2 :]
-    outs, parts, (g_ref, total, sems) = refs[:n], refs[n : n + PARTS - 1], refs[n + PARTS - 1 :]
-    part, width = parts[0].shape
-    rows, columns = min(part, 256), min(width, 256)
-    tiles = [(p, i) for p in range(PARTS - 1) for i in range(part // rows)]
-
-    def copy(k):
-        p, i = tiles[k]
-        return pltpu.make_async_copy(
-            b_ref.at[pl.ds((p + 1) * part + i * rows, rows), :], parts[p].at[pl.ds(i * rows, rows), :], sems.at[k]
-        )
-
-    def copy_at(p, i):
-        return pltpu.make_async_copy(
-            b_ref.at[span((p + 1) * (part // rows) + i, rows), :],
-            parts[p].at[span(i, rows), :],
-            sems.at[p * (part // rows) + i],
-        )
-
-    for k in range(len(tiles)):
-        copy(k).start()
+    outs, parts, (g_ref, total, sems) = refs[:n], refs[n : n + len(PARTS) - 1], refs[n + len(PARTS) - 1 :]
+    width = ready.shape[1]
+    rows, columns = b_ref.shape[0] // 16, min(width, 256)
+    begins = [sum(PARTS[:p]) for p in range(len(PARTS))]
+
+    def copy(p, i):
+        k = begins[p] + i
+        return pltpu.make_async_copy(b_ref.at[span(k, rows), :], parts[p - 1].at[span(i, rows), :], sems.at[k])
+
+    for p in range(1, len(PARTS)):
+        for i in range(PARTS[p]):
+            copy(p, i).start()
     g_ref[...] = jnp.concatenate([block[...].astype(F32) for block in blocks], axis=0).astype(BF16)
     total[...] = jnp.zeros_like(total)
     for p, ref in enumerate((ready, *parts)):
 
         def tile(i, _, p=p, ref=ref):
             if p:
-                copy_at(p - 1, i).wait()
-            g = g_ref[:, pl.ds(pl.multiple_of(p * part + i * rows, rows), rows)]
+                copy(p, i).wait()
+            g = g_ref[:, span(begins[p] + i, rows)]
             for j in range(width // columns):
                 at = slice(j * columns, (j + 1) * columns)
                 high, low = split(ref[span(i, rows), at])
@@ -131,7 +123,7 @@
                 )
             return 0
 
-        lax.fori_loop(0, part // rows, tile, 0)
+        lax.fori_loop(0, PARTS[p], tile, 0)
     pair = blocks[0].shape[0]
     chip = lax.axis_index("rows") // 2
     each = chips // n
@@ -162,24 +154,18 @@
         x_ref[span(lax.axis_index("cols") ^ s, each), :] = block[...]
     high, low = split(x_ref[...])
     x2_ref[:rows, :], x2_ref[rows:, :] = high, low
-    part = rest[0].shape[0]
-    size = min(part, 512)
-
-    def store(to, first, second):
-        o_ref[:, to : to + size] = first[:rows] + first[rows:] + second
+    begins = [sum(PARTS[:p]) * o_ref.shape[1] // 16 for p in range(len(PARTS) + 1)]
+
+    def store(p, first, second):
+        o_ref[:, begins[p] : begins[p + 1]] = first[:rows] + first[rows:] + second
 
     for p, (high, low) in enumerate(zip(pieces[::2], pieces[1::2])):
-        for i in range(part // size):
-            at = slice(i * size, (i + 1) * size)
-            first = jnp.dot(x2_ref[...], high[:, at], preferred_element_type=F32)
-            second = jnp.dot(x2_ref[:rows, :], low[:, at], preferred_element_type=F32)
-            store(p * part + i * size, first, second)
-    for p, ref in enumerate(rest):
-        for i in range(part // size):
-            high, low = split(ref[i * size : (i + 1) * size, :])
-            first = lax.dot_general(x2_ref[...], high, TRANSPOSED, preferred_element_type=F32)
-            second = lax.dot_general(x2_ref[:rows, :], low, TRANSPOSED, preferred_element_type=F32)
-            store((len(pieces) // 2 + p) * part + i * size, first, second)
+        first = jnp.dot(x2_ref[...], high[...], preferred_element_type=F32)
+        store(p, first, jnp.dot(x2_ref[:rows, :], low[...], preferred_element_type=F32))
+    for p, ref in enumerate(rest, len(pieces) // 2):
+        high, low = split(ref[...])
+        first = lax.dot_general(x2_ref[...], high, TRANSPOSED, preferred_element_type=F32)
+        store(p, first, lax.dot_general(x2_ref[:rows, :], low, TRANSPOSED, preferred_element_type=F32))
     odd = lax.rem(lax.axis_index("rows"), 2) == 1
     chips, four, height = keep.shape
     whole = o_ref[...].reshape(chips, 2, four, height)
@@ -202,8 +188,8 @@
     chips = m // 2
     each, width = moment.shape
     four, height = gradient.shape
-    part = height // PARTS
-    partbytes = part * width * 4
+    sizes = [share * height // 16 for share in PARTS]
+    moved = height * width * 4
 
     def along(x, axis, size, s):
         return lax.ppermute(x, axis, [(i, i ^ s) for i in range(size)])
@@ -228,30 +214,30 @@
     from_chips = [own] + [along_rows(own, 2 * s) for s in range(1, chips)]
     first = kernel(
         load_kernel,
-        pltpu.VMEM((part, width), F32),
+        pltpu.VMEM((sizes[0], width), F32),
         [ANY, FAR],
         (own, basis),
         [pltpu.SemaphoreType.DMA((4,))],
-        2 * partbytes,
+        moved // 2,
     )
     results = kernel(
         functools.partial(rotate_kernel, n, chips),
-        [f32(each, width)] * n + [pltpu.VMEM((part, width), F32)] * (PARTS - 1),
+        [f32(each, width)] * n + [pltpu.VMEM((size, width), F32) for size in sizes[1:]],
         [WHOLE] * (chips + 1) + [FAR],
         (*from_chips, first, basis),
         [
             pltpu.VMEM((n * each, height), BF16),
             pltpu.VMEM((n * each, width), F32),
-            pltpu.SemaphoreType.DMA((height // min(part, 256),)),
+            pltpu.SemaphoreType.DMA((16,)),
         ],
-        PARTS * partbytes,
+        moved,
     )
     parts, (early, later, *rest) = results[:n], [
         pltpu.with_memory_space_constraint(x, pltpu.VMEM) for x in (first, *results[n:])
     ]
     parts = [parts[0]] + [along_cols(parts[s], s) for s in range(1, n)]
     pieces = list(
-        kernel(turn_kernel, turned(part, width), [WHOLE] * (2 + len(rest)), (early, later, *rest), (), 2 * partbytes)
+        kernel(turn_kernel, turned(sizes[0], width), [WHOLE] * (2 + len(rest)), (early, later, *rest), (), moved // 2)
     )
     pieces = [pltpu.with_memory_space_constraint(x, pltpu.VMEM) for x in pieces]
     normed, rotated = kernel(
@@ -264,7 +250,7 @@
         moments_kernel, [f32(each, width)] * 2, [WHOLE] * 3, (moment, second, rotated), (), 8 * each * width * 4
     )
     blocks = [normed] + [along_cols(normed, s) for s in range(1, n)]
-    pieces += list(kernel(turn_kernel, turned(part, width), [WHOLE] * (1 + len(rest)), (later, *rest), (), 2 * partbytes))
+    pieces += list(kernel(turn_kernel, turned(sizes[1], width), [WHOLE] * (1 + len(rest)), (later, *rest), (), moved // 2))
     keep, send = kernel(
         functools.partial(back_kernel, n, len(pieces)),
         [f32(chips, four, height)] * 2,
@@ -275,7 +261,7 @@
             pltpu.VMEM((2 * n * each, width), BF16),
             pltpu.VMEM((n * each, height), F32),
         ],
-        PARTS * partbytes,
+        moved,
     )
     got = along_rows(send, 1)
     halves = kernel(fold_kernel, [f32(four, height)] * chips, [WHOLE] * 2, (keep, got))

time: 56.3 us -> 55.7 us (0.989)
  waiting for transfers between devices: 10.2 us -> 9.46 us
    ppermute x14, waiting for transfers between devices: 10.2 us -> 9.46 us  [along(): return lax.ppermute(x, axis, [(i, i ^ s) for i in range(size)])]
  transfers between devices with their start and end apart: 14 -> 14, of which waited for: 10 -> 8; matrix products, arithmetic and copies ran while one was open for 0% -> 0% of each run, Pallas kernels for 18% -> 20%
where the time goes in v4:
time: 55.7 us; the launch traced here: 55.5 us
  Pallas kernels  26.9 us (48%)
  starting transfers between devices  17.8 us (32%)
  waiting for transfers between devices  9.46 us (17%)
  between operations  0.75 us (1%)
  other arithmetic  0.67 us (1%)
    pallas_call x10, Pallas kernels, kernel(): pl.pallas_call(body, out_shape=outs, in_specs=ins, out_specs=jax.tree.map...  26.9 us
    ppermute x14, starting transfers between devices, along(): return lax.ppermute(x, axis, [(i, i ^ s) for i in range(size)])  17.8 us
    ppermute x14, waiting for transfers between devices, along(): return lax.ppermute(x, axis, [(i, i ^ s) for i in range(size)])  9.46 us
  transfers between devices with their start and end apart: 14, of which 8 were waited for; matrix products, arithmetic and copies ran while one was open for 0% of the time, Pallas kernels for 20%

profile of v4, /device:TPU:0, one launch (start us, length us, event | category | flops | bytes accessed | tf_op | source)
XLA Modules:
  0.0 55.5 jit_solution(12799970168599282421)
XLA Ops:
  0.6 0.6 %collective-permute-start = (bf16[4,4096]{1,0:T(4,128)(2,1)}, bf16[4,4096]{1,0:T(4,128)(2,1)S(1)}, u32[]{:S(2)}, u32[]{:S(2)}) collective-permute-start(bf16[4,4096]{1,0:T(4,128)(2,1)} %far.1), channel_id=1, source_target_pairs={{0,4},{4,0},{8,12},{12,8},{16,20},{20,16},{24,28},{28,24},{1,5},{5... | collective-permute-start | bytes 98312 | tf_op jit(solution)/shard_map/ppermute | solution.py:195
  1.2 0.8 %shard_map.67.own = bf16[4,4096]{1,0:T(4,128)(2,1)S(1)} custom-call(bf16[4,4096]{1,0:T(4,128)(2,1)} %far.1), custom_call_target="tpu_custom_call" | custom-call | bytes 65536 | tf_op jit(solution)/shard_map/pallas_call | solution.py:28
  2.0 0.3 collective-permute-done.got
  2.3 3.8 %collective-permute-start.3 = (bf16[8,4096]{1,0:T(8,128)(2,1)S(1)}, bf16[8,4096]{1,0:T(8,128)(2,1)S(1)}, u32[]{:S(2)}, u32[]{:S(2)}) collective-permute-start(bf16[8,4096]{1,0:T(8,128)(2,1)S(1)} %shard_map.68._.refs_0_), channel_id=1, source_target_pairs={{0,24},{4,28},{8,16},{12,20},{16,8},{20,12},{24,0},{28,4},{1,25},{... | collective-permute-start | bytes 196616 | tf_op jit(solution)/shard_map/ppermute | solution.py:195
  6.1 0.5 collective-permute-start.2
  6.6 0.1 collective-permute-start.1
  6.8 4.1 %shard_map.69.refs_4_.b_ref = f32[1280,2048]{1,0:T(8,128)S(1)} custom-call(bf16[8,4096]{1,0:T(8,128)(2,1)S(1)} %shard_map.68._.refs_0_, f32[4096,2048]{1,0:T(8,128)} %refs_5_.1), custom_call_target="tpu_custom_call" | custom-call | bytes 16777216 | tf_op jit(solution)/shard_map/pallas_call | solution.py:28
  10.9 0.0 collective-permute-done.3.refs_3_
  10.9 0.0 collective-permute-done.1.refs_1_
  10.9 8.3 %shard_map.70 = (f32[8,2048]{1,0:T(8,128)S(1)}, f32[8,2048]{1,0:T(8,128)S(1)}, f32[8,2048]{1,0:T(8,128)S(1)}, f32[8,2048]{1,0:T(8,128)S(1)}, f32[1280,2048]{1,0:...) custom-call(bf16[8,4096]{1,0:T(8,128)(2,1)S(1)} %shard_map.68._.refs_0_, ...), custom_call_target="tpu_custom_call" | custom-call | bytes 33554432 | tf_op jit(solution)/shard_map/pallas_call | solution.py:28
  19.2 2.0 %collective-permute-start.4 = (f32[8,2048]{1,0:T(8,128)S(1)}, f32[8,2048]{1,0:T(8,128)S(1)}, u32[]{:S(2)}, u32[]{:S(2)}) collective-permute-start(f32[8,2048]{1,0:T(8,128)S(1)} %get-tuple-element.25), channel_id=1, source_target_pairs={{0,1},{1,0},{2,3},{3,2},{4,5},{5,4},{6,7},{7,6},{8,9},{9,8},{10,11... | collective-permute-start | bytes 196616 | tf_op jit(solution)/shard_map/ppermute | solution.py:195
  21.3 2.6 %collective-permute-start.5 = (f32[8,2048]{1,0:T(8,128)S(1)}, f32[8,2048]{1,0:T(8,128)S(1)}, u32[]{:S(2)}, u32[]{:S(2)}) collective-permute-start(f32[8,2048]{1,0:T(8,128)S(1)} %get-tuple-element.26), channel_id=1, source_target_pairs={{0,2},{1,3},{2,0},{3,1},{4,6},{5,7},{6,4},{7,5},{8,10},{9,11},{10,... | collective-permute-start | bytes 196616 | tf_op jit(solution)/shard_map/ppermute | solution.py:195
  23.9 2.7 %shard_map.71 = (bf16[2048,1280]{1,0:T(8,128)(2,1)S(1)}, bf16[2048,1280]{1,0:T(8,128)(2,1)S(1)}) custom-call(f32[1280,2048]{1,0:T(8,128)S(1)} %shard_map.69.refs_4_.b_ref, f32[1280,2048]{1,0:T(8,128)S(1)} %get-tuple-element.28.refs_0_.refs_6_.b_ref, f32[768,2048]{1,0:T(8,128)S(1)} %get-tuple-element.29.refs_1_.refs_7_.refs_0_.refs_8_, ...), custom_call_target="tpu_custom_call" | custom-call | bytes 16777216 | tf_op jit(solution)/shard_map/pallas_call | solution.py:28
  26.6 1.4 %collective-permute-done.5.refs_2_ = f32[8,2048]{1,0:T(8,128)S(1)} collective-permute-done((f32[8,2048]{1,0:T(8,128)S(1)}, f32[8,2048]{1,0:T(8,128)S(1)}, u32[]{:S(2)}, u32[]{:S(2)}) %collective-permute-start.5) | collective-permute-done | bytes 65568 | tf_op jit(solution)/shard_map/ppermute | solution.py:195
  28.0 1.9 %collective-permute-done.6.refs_3_ = f32[8,2048]{1,0:T(8,128)S(1)} collective-permute-done((f32[8,2048]{1,0:T(8,128)S(1)}, f32[8,2048]{1,0:T(8,128)S(1)}, u32[]{:S(2)}, u32[]{:S(2)}) %collective-permute-start.6) | collective-permute-done | bytes 65568 | tf_op jit(solution)/shard_map/ppermute | solution.py:195
  29.9 0.1 shard_map.72
  30.0 1.3 %collective-permute-start.9 = (f32[8,2048]{1,0:T(8,128)S(1)}, f32[8,2048]{1,0:T(8,128)S(1)}, u32[]{:S(2)}, u32[]{:S(2)}) collective-permute-start(f32[8,2048]{1,0:T(8,128)S(1)} %get-tuple-element.33.refs_0_), channel_id=1, source_target_pairs={{0,3},{1,2},{2,1},{3,0},{4,7},{5,6},{6,5},{7,4},{8,11},{9,10},{10,... | collective-permute-start | bytes 196616 | tf_op jit(solution)/shard_map/ppermute | solution.py:195
  31.3 3.1 %collective-permute-start.7 = (f32[8,2048]{1,0:T(8,128)S(1)}, f32[8,2048]{1,0:T(8,128)S(1)}, u32[]{:S(2)}, u32[]{:S(2)}) collective-permute-start(f32[8,2048]{1,0:T(8,128)S(1)} %get-tuple-element.33.refs_0_), channel_id=1, source_target_pairs={{0,1},{1,0},{2,3},{3,2},{4,5},{5,4},{6,7},{7,6},{8,9},{9,8},{10,11... | collective-permute-start | bytes 196616 | tf_op jit(solution)/shard_map/ppermute | solution.py:195
  34.4 2.7 %shard_map.73 = (bf16[2048,1280]{1,0:T(8,128)(2,1)S(1)}, bf16[2048,1280]{1,0:T(8,128)(2,1)S(1)}) custom-call(f32[1280,2048]{1,0:T(8,128)S(1)} %get-tuple-element.28.refs_0_.refs_6_.b_ref, f32[768,2048]{1,0:T(8,128)S(1)} %get-tuple-element.29.refs_1_.refs_7_.refs_0_.refs_8_, f32[768,2048]{1,0:T(8,128)S(1)} %get-tuple-element.30.refs_2_.refs_8_.refs_1_.refs_9_), custom_call_target="tpu_custom_call" | custom-call | bytes 16777216 | tf_op jit(solution)/shard_map/pallas_call | solution.py:28
  37.2 0.3 collective-permute-done.8.refs_2_
  37.5 7.4 %shard_map.74 = (f32[4,4,4096]{2,1,0:T(4,128)S(1)}, f32[4,4,4096]{2,1,0:T(4,128)S(1)}) custom-call(f32[8,2048]{1,0:T(8,128)S(1)} %get-tuple-element.33.refs_0_, f32[8,2048]{1,0:T(8,128)S(1)} %collective-permute-done.7.refs_1_, f32[8,2048]{1,0:T(8,128)S(1)} %collective-permute-done.8.refs_2_, f32[8,2048]{1,0:T(8,128)S(1)} %collective-permute-done.9.refs_3_, ...), custom_call_target="tpu_custom_call" | custom-call | bytes 33554432 | tf_op jit(solution)/shard_map/pallas_call | solution.py:28
  44.9 0.1 collective-permute-start.10
  45.0 1.5 %collective-permute-done.10.got = f32[4,4,4096]{2,1,0:T(4,128)S(1)} collective-permute-done((f32[4,4,4096]{2,1,0:T(4,128)S(1)}, f32[4,4,4096]{2,1,0:T(4,128)S(1)}, u32[]{:S(2)}, u32[]{:S(2)}) %collective-permute-start.10) | collective-permute-done | bytes 262176 | tf_op jit(solution)/shard_map/ppermute | solution.py:195
  46.5 0.1 shard_map.75
  46.6 1.6 %collective-permute-start.11 = (f32[4,4096]{1,0:T(4,128)S(1)}, f32[4,4096]{1,0:T(4,128)S(1)}, u32[]{:S(2)}, u32[]{:S(2)}) collective-permute-start(f32[4,4096]{1,0:T(4,128)S(1)} %get-tuple-element.39), channel_id=1, source_target_pairs={{0,8},{4,12},{8,0},{12,4},{16,24},{20,28},{24,16},{28,20},{1,9},{5... | collective-permute-start | bytes 196616 | tf_op jit(solution)/shard_map/ppermute | solution.py:195
  48.1 1.5 %collective-permute-start.12 = (f32[4,4096]{1,0:T(4,128)S(1)}, f32[4,4096]{1,0:T(4,128)S(1)}, u32[]{:S(2)}, u32[]{:S(2)}) collective-permute-start(f32[4,4096]{1,0:T(4,128)S(1)} %get-tuple-element.40), channel_id=1, source_target_pairs={{0,16},{4,20},{8,24},{12,28},{16,0},{20,4},{24,8},{28,12},{1,17},{... | collective-permute-start | bytes 196616 | tf_op jit(solution)/shard_map/ppermute | solution.py:195
  49.7 0.5 collective-permute-start.13
  50.1 0.7 %shard_map.76 = (f32[8,2048]{1,0:T(8,128)}, f32[8,2048]{1,0:T(8,128)}) custom-call(f32[8,2048]{1,0:T(8,128)S(1)} %copy-done, f32[8,2048]{1,0:T(8,128)S(1)} %copy-done.1, f32[8,2048]{1,0:T(8,128)S(1)} %get-tuple-element.42.rotated), custom_call_target="tpu_custom_call" | custom-call | bytes 524288 | tf_op jit(solution)/shard_map/pallas_call | solution.py:28
  50.8 0.1 collective-permute-done.11
  50.9 1.5 %collective-permute-done.12 = f32[4,4096]{1,0:T(4,128)S(1)} collective-permute-done((f32[4,4096]{1,0:T(4,128)S(1)}, f32[4,4096]{1,0:T(4,128)S(1)}, u32[]{:S(2)}, u32[]{:S(2)}) %collective-permute-start.12) | collective-permute-done | bytes 65568 | tf_op jit(solution)/shard_map/ppermute | solution.py:195
  52.4 2.4 %collective-permute-done.13 = f32[4,4096]{1,0:T(4,128)S(1)} collective-permute-done((f32[4,4096]{1,0:T(4,128)S(1)}, f32[4,4096]{1,0:T(4,128)S(1)}, u32[]{:S(2)}, u32[]{:S(2)}) %collective-permute-start.13) | collective-permute-done | bytes 65568 | tf_op jit(solution)/shard_map/ppermute | solution.py:195
  54.8 0.7 %add_add_fusion = f32[4,4096]{1,0:T(4,128)} fusion(f32[4,4096]{1,0:T(4,128)S(1)} %collective-permute-done.13, f32[4,4096]{1,0:T(4,128)S(1)} %collective-permute-done.12, f32[4,4096]{1,0:T(4,128)S(1)} %get-tuple-element.38, f32[4,4096]{1,0:T(4,128)S(1)} %collective-permute-done.11), kind=kLoop, calls=%fused_computation | loop fusion | flops 49152 | bytes 327680 | tf_op jit(solution)/shard_map/add | solution.py:270
  (11 shorter events, 0.0 us)
Async XLA Ops:
  0.6 1.6 %collective-permute-start = (bf16[4,4096]{1,0:T(4,128)(2,1)}, bf16[4,4096]{1,0:T(4,128)(2,1)S(1)}, u32[]{:S(2)}, u32[]{:S(2)}) collective-permute-start(bf16[4,4096]{1,0:T(4,128)(2,1)} %far.1), channel_id=1, source_target_pairs={{0,4},{4,0},{8,12},{12,8},{16,20},{20,16},{24,28},{28,24},{1,5},{5... | collective-permute-start | bytes 98312 | tf_op jit(solution)/shard_map/ppermute | solution.py:195
  2.3 8.6 %collective-permute-start.3 = (bf16[8,4096]{1,0:T(8,128)(2,1)S(1)}, bf16[8,4096]{1,0:T(8,128)(2,1)S(1)}, u32[]{:S(2)}, u32[]{:S(2)}) collective-permute-start(bf16[8,4096]{1,0:T(8,128)(2,1)S(1)} %shard_map.68._.refs_0_), channel_id=1, source_target_pairs={{0,24},{4,28},{8,16},{12,20},{16,8},{20,12},{24,0},{28,4},{1,25},{... | collective-permute-start | bytes 196616 | tf_op jit(solution)/shard_map/ppermute | solution.py:195
  6.1 4.8 %collective-permute-start.2 = (bf16[8,4096]{1,0:T(8,128)(2,1)S(1)}, bf16[8,4096]{1,0:T(8,128)(2,1)S(1)}, u32[]{:S(2)}, u32[]{:S(2)}) collective-permute-start(bf16[8,4096]{1,0:T(8,128)(2,1)S(1)} %shard_map.68._.refs_0_), channel_id=1, source_target_pairs={{0,16},{4,20},{8,24},{12,28},{16,0},{20,4},{24,8},{28,12},{1,17},{... | collective-permute-start | bytes 196616 | tf_op jit(solution)/shard_map/ppermute | solution.py:195
  6.6 4.3 %collective-permute-start.1 = (bf16[8,4096]{1,0:T(8,128)(2,1)S(1)}, bf16[8,4096]{1,0:T(8,128)(2,1)S(1)}, u32[]{:S(2)}, u32[]{:S(2)}) collective-permute-start(bf16[8,4096]{1,0:T(8,128)(2,1)S(1)} %shard_map.68._.refs_0_), channel_id=1, source_target_pairs={{0,8},{4,12},{8,0},{12,4},{16,24},{20,28},{24,16},{28,20},{1,9},{5... | collective-permute-start | bytes 196616 | tf_op jit(solution)/shard_map/ppermute | solution.py:195
  19.2 7.4 %collective-permute-start.4 = (f32[8,2048]{1,0:T(8,128)S(1)}, f32[8,2048]{1,0:T(8,128)S(1)}, u32[]{:S(2)}, u32[]{:S(2)}) collective-permute-start(f32[8,2048]{1,0:T(8,128)S(1)} %get-tuple-element.25), channel_id=1, source_target_pairs={{0,1},{1,0},{2,3},{3,2},{4,5},{5,4},{6,7},{7,6},{8,9},{9,8},{10,11... | collective-permute-start | bytes 196616 | tf_op jit(solution)/shard_map/ppermute | solution.py:195
  21.3 6.7 %collective-permute-start.5 = (f32[8,2048]{1,0:T(8,128)S(1)}, f32[8,2048]{1,0:T(8,128)S(1)}, u32[]{:S(2)}, u32[]{:S(2)}) collective-permute-start(f32[8,2048]{1,0:T(8,128)S(1)} %get-tuple-element.26), channel_id=1, source_target_pairs={{0,2},{1,3},{2,0},{3,1},{4,6},{5,7},{6,4},{7,5},{8,10},{9,11},{10,... | collective-permute-start | bytes 196616 | tf_op jit(solution)/shard_map/ppermute | solution.py:195
  23.9 6.1 %collective-permute-start.6 = (f32[8,2048]{1,0:T(8,128)S(1)}, f32[8,2048]{1,0:T(8,128)S(1)}, u32[]{:S(2)}, u32[]{:S(2)}) collective-permute-start(f32[8,2048]{1,0:T(8,128)S(1)} %get-tuple-element.27), channel_id=1, source_target_pairs={{0,3},{1,2},{2,1},{3,0},{4,7},{5,6},{6,5},{7,4},{8,11},{9,10},{10,... | collective-permute-start | bytes 196616 | tf_op jit(solution)/shard_map/ppermute | solution.py:195
  23.9 6.1 %copy-start = (f32[8,2048]{1,0:T(8,128)S(1)}, f32[8,2048]{1,0:T(8,128)}, u32[]{:S(2)}) copy-start(f32[8,2048]{1,0:T(8,128)} %m_ref.3) | copy-start | bytes 196612
  23.9 6.1 %copy-start.1 = (f32[8,2048]{1,0:T(8,128)S(1)}, f32[8,2048]{1,0:T(8,128)}, u32[]{:S(2)}) copy-start(f32[8,2048]{1,0:T(8,128)} %s_ref.3) | copy-start | bytes 196612
  30.0 7.2 %collective-permute-start.9 = (f32[8,2048]{1,0:T(8,128)S(1)}, f32[8,2048]{1,0:T(8,128)S(1)}, u32[]{:S(2)}, u32[]{:S(2)}) collective-permute-start(f32[8,2048]{1,0:T(8,128)S(1)} %get-tuple-element.33.refs_0_), channel_id=1, source_target_pairs={{0,3},{1,2},{2,1},{3,0},{4,7},{5,6},{6,5},{7,4},{8,11},{9,10},{10,... | collective-permute-start | bytes 196616 | tf_op jit(solution)/shard_map/ppermute | solution.py:195
  31.3 6.2 %collective-permute-start.8 = (f32[8,2048]{1,0:T(8,128)S(1)}, f32[8,2048]{1,0:T(8,128)S(1)}, u32[]{:S(2)}, u32[]{:S(2)}) collective-permute-start(f32[8,2048]{1,0:T(8,128)S(1)} %get-tuple-element.33.refs_0_), channel_id=1, source_target_pairs={{0,2},{1,3},{2,0},{3,1},{4,6},{5,7},{6,4},{7,5},{8,10},{9,11},{10,... | collective-permute-start | bytes 196616 | tf_op jit(solution)/shard_map/ppermute | solution.py:195
  31.3 6.2 %collective-permute-start.7 = (f32[8,2048]{1,0:T(8,128)S(1)}, f32[8,2048]{1,0:T(8,128)S(1)}, u32[]{:S(2)}, u32[]{:S(2)}) collective-permute-start(f32[8,2048]{1,0:T(8,128)S(1)} %get-tuple-element.33.refs_0_), channel_id=1, source_target_pairs={{0,1},{1,0},{2,3},{3,2},{4,5},{5,4},{6,7},{7,6},{8,9},{9,8},{10,11... | collective-permute-start | bytes 196616 | tf_op jit(solution)/shard_map/ppermute | solution.py:195
  44.9 1.6 %collective-permute-start.10 = (f32[4,4,4096]{2,1,0:T(4,128)S(1)}, f32[4,4,4096]{2,1,0:T(4,128)S(1)}, u32[]{:S(2)}, u32[]{:S(2)}) collective-permute-start(f32[4,4,4096]{2,1,0:T(4,128)S(1)} %get-tuple-element.37), channel_id=1, source_target_pairs={{0,4},{4,0},{8,12},{12,8},{16,20},{20,16},{24,28},{28,24},{1,5},{5... | collective-permute-start | bytes 786440 | tf_op jit(solution)/shard_map/ppermute | solution.py:195
  46.6 4.3 %collective-permute-start.11 = (f32[4,4096]{1,0:T(4,128)S(1)}, f32[4,4096]{1,0:T(4,128)S(1)}, u32[]{:S(2)}, u32[]{:S(2)}) collective-permute-start(f32[4,4096]{1,0:T(4,128)S(1)} %get-tuple-element.39), channel_id=1, source_target_pairs={{0,8},{4,12},{8,0},{12,4},{16,24},{20,28},{24,16},{28,20},{1,9},{5... | collective-permute-start | bytes 196616 | tf_op jit(solution)/shard_map/ppermute | solution.py:195
  48.1 4.3 %collective-permute-start.12 = (f32[4,4096]{1,0:T(4,128)S(1)}, f32[4,4096]{1,0:T(4,128)S(1)}, u32[]{:S(2)}, u32[]{:S(2)}) collective-permute-start(f32[4,4096]{1,0:T(4,128)S(1)} %get-tuple-element.40), channel_id=1, source_target_pairs={{0,16},{4,20},{8,24},{12,28},{16,0},{20,4},{24,8},{28,12},{1,17},{... | collective-permute-start | bytes 196616 | tf_op jit(solution)/shard_map/ppermute | solution.py:195
  49.7 5.2 %collective-permute-start.13 = (f32[4,4096]{1,0:T(4,128)S(1)}, f32[4,4096]{1,0:T(4,128)S(1)}, u32[]{:S(2)}, u32[]{:S(2)}) collective-permute-start(f32[4,4096]{1,0:T(4,128)S(1)} %get-tuple-element.41), channel_id=1, source_target_pairs={{0,24},{4,28},{8,16},{12,20},{16,8},{20,12},{24,0},{28,4},{1,25},{... | collective-permute-start | bytes 196616 | tf_op jit(solution)/shard_map/ppermute | solution.py:195

commit v5 on v4

--- a/solution.py
+++ b/solution.py
@@ -11,7 +11,6 @@
 WHOLE = pl.BlockSpec(memory_space=pltpu.VMEM)
 FAR = pl.BlockSpec(memory_space=pltpu.HBM)
 ANY = pl.BlockSpec(memory_space=pl.ANY)
-TRANSPOSED = (((1,), (1,)), ((), ()))
 LIMIT = 6 << 20
 PARTS = (5, 5, 3, 3)
 
@@ -147,8 +146,8 @@
 
 
 def back_kernel(n, kept, *refs):
-    blocks, pieces, rest = refs[:n], refs[n : n + kept], refs[n + kept : -5]
-    keep, send, x_ref, x2_ref, o_ref = refs[-5:]
+    blocks, pieces, rest = refs[:n], refs[n : n + kept], refs[n + kept : -7]
+    keep, send, x_ref, x2_ref, o_ref, turned_high, turned_low = refs[-7:]
     each, rows = blocks[0].shape[0], x_ref.shape[0]
     for s, block in enumerate(blocks):
         x_ref[span(lax.axis_index("cols") ^ s, each), :] = block[...]
@@ -156,16 +155,29 @@
     x2_ref[:rows, :], x2_ref[rows:, :] = high, low
     begins = [sum(PARTS[:p]) * o_ref.shape[1] // 16 for p in range(len(PARTS) + 1)]
 
-    def store(p, first, second):
-        o_ref[:, begins[p] : begins[p + 1]] = first[:rows] + first[rows:] + second
-
-    for p, (high, low) in enumerate(zip(pieces[::2], pieces[1::2])):
-        first = jnp.dot(x2_ref[...], high[...], preferred_element_type=F32)
-        store(p, first, jnp.dot(x2_ref[:rows, :], low[...], preferred_element_type=F32))
-    for p, ref in enumerate(rest, len(pieces) // 2):
-        high, low = split(ref[...])
-        first = lax.dot_general(x2_ref[...], high, TRANSPOSED, preferred_element_type=F32)
-        store(p, first, lax.dot_general(x2_ref[:rows, :], low, TRANSPOSED, preferred_element_type=F32))
+    size = o_ref.shape[1] // 16
+
+    def multiply(to, high, low):
+        first = jnp.dot(x2_ref[...], high, preferred_element_type=F32)
+        second = jnp.dot(x2_ref[:rows, :], low, preferred_element_type=F32)
+        o_ref[:, to : to + size] = first[:rows] + first[rows:] + second
+
+    ready = [
+        (begins[p] + i * size, high, low, i)
+        for p, (high, low) in enumerate(zip(pieces[::2], pieces[1::2]))
+        for i in range(PARTS[p])
+    ]
+    waiting = [
+        (begins[p] + i * size, ref, i) for p, ref in enumerate(rest, len(pieces) // 2) for i in range(PARTS[p])
+    ]
+    slots = turned_high.shape[0]
+    for k, (_, ref, i) in enumerate(waiting):
+        turn(lambda at, ref=ref, i=i: ref[i * size : (i + 1) * size, at], turned_high.at[k % slots], turned_low.at[k % slots], 0, size)
+        for to, high, low, j in ready[k * len(ready) // len(waiting) : (k + 1) * len(ready) // len(waiting)]:
+            multiply(to, high[:, j * size : (j + 1) * size], low[:, j * size : (j + 1) * size])
+        if k:
+            multiply(waiting[k - 1][0], turned_high[(k - 1) % slots], turned_low[(k - 1) % slots])
+    multiply(waiting[-1][0], turned_high[(len(waiting) - 1) % slots], turned_low[(len(waiting) - 1) % slots])
     odd = lax.rem(lax.axis_index("rows"), 2) == 1
     chips, four, height = keep.shape
     whole = o_ref[...].reshape(chips, 2, four, height)
@@ -260,6 +272,8 @@
             pltpu.VMEM((n * each, width), F32),
             pltpu.VMEM((2 * n * each, width), BF16),
             pltpu.VMEM((n * each, height), F32),
+            pltpu.VMEM((2, width, height // 16), BF16),
+            pltpu.VMEM((2, width, height // 16), BF16),
         ],
         moved,
     )

time: 55.7 us -> 54.4 us (0.977)
  Pallas kernels: 26.9 us -> 25.6 us
    pallas_call x10, Pallas kernels: 26.9 us -> 25.6 us  [kernel(): pl.pallas_call(body, out_shape=outs, in_specs=ins, out_specs=jax.tree.map...]
where the time goes in v5:
time: 54.4 us; the launch traced here: 54.2 us
  Pallas kernels  25.6 us (47%)
  starting transfers between devices  17.8 us (33%)
  waiting for transfers between devices  9.45 us (17%)
  between operations  0.74 us (1%)
  other arithmetic  0.67 us (1%)
    pallas_call x10, Pallas kernels, kernel(): pl.pallas_call(body, out_shape=outs, in_specs=ins, out_specs=jax.tree.map...  25.6 us
    ppermute x14, starting transfers between devices, along(): return lax.ppermute(x, axis, [(i, i ^ s) for i in range(size)])  17.8 us
    ppermute x14, waiting for transfers between devices, along(): return lax.ppermute(x, axis, [(i, i ^ s) for i in range(size)])  9.45 us
  transfers between devices with their start and end apart: 14, of which 8 were waited for; matrix products, arithmetic and copies ran while one was open for 0% of the time, Pallas kernels for 20%

profile of v5, /device:TPU:0, one launch (start us, length us, event | category | flops | bytes accessed | tf_op | source)
XLA Modules:
  0.0 54.2 jit_solution(12912185293637680209)
XLA Ops:
  0.6 0.6 %collective-permute-start = (bf16[4,4096]{1,0:T(4,128)(2,1)}, bf16[4,4096]{1,0:T(4,128)(2,1)S(1)}, u32[]{:S(2)}, u32[]{:S(2)}) collective-permute-start(bf16[4,4096]{1,0:T(4,128)(2,1)} %far.1), channel_id=1, source_target_pairs={{0,4},{4,0},{8,12},{12,8},{16,20},{20,16},{24,28},{28,24},{1,5},{5... | collective-permute-start | bytes 98312 | tf_op jit(solution)/shard_map/ppermute | solution.py:207
  1.2 0.8 %shard_map.67.own = bf16[4,4096]{1,0:T(4,128)(2,1)S(1)} custom-call(bf16[4,4096]{1,0:T(4,128)(2,1)} %far.1), custom_call_target="tpu_custom_call" | custom-call | bytes 65536 | tf_op jit(solution)/shard_map/pallas_call | solution.py:27
  2.0 0.3 collective-permute-done.got
  2.3 3.8 %collective-permute-start.3 = (bf16[8,4096]{1,0:T(8,128)(2,1)S(1)}, bf16[8,4096]{1,0:T(8,128)(2,1)S(1)}, u32[]{:S(2)}, u32[]{:S(2)}) collective-permute-start(bf16[8,4096]{1,0:T(8,128)(2,1)S(1)} %shard_map.68._.refs_0_), channel_id=1, source_target_pairs={{0,24},{4,28},{8,16},{12,20},{16,8},{20,12},{24,0},{28,4},{1,25},{... | collective-permute-start | bytes 196616 | tf_op jit(solution)/shard_map/ppermute | solution.py:207
  6.1 0.5 collective-permute-start.2
  6.6 0.1 collective-permute-start.1
  6.8 4.1 %shard_map.69.refs_4_.b_ref = f32[1280,2048]{1,0:T(8,128)S(1)} custom-call(bf16[8,4096]{1,0:T(8,128)(2,1)S(1)} %shard_map.68._.refs_0_, f32[4096,2048]{1,0:T(8,128)} %refs_5_.1), custom_call_target="tpu_custom_call" | custom-call | bytes 16777216 | tf_op jit(solution)/shard_map/pallas_call | solution.py:27
  10.9 0.0 collective-permute-done.3.refs_3_
  10.9 0.0 collective-permute-done.1.refs_1_
  10.9 8.3 %shard_map.70 = (f32[8,2048]{1,0:T(8,128)S(1)}, f32[8,2048]{1,0:T(8,128)S(1)}, f32[8,2048]{1,0:T(8,128)S(1)}, f32[8,2048]{1,0:T(8,128)S(1)}, f32[1280,2048]{1,0:...) custom-call(bf16[8,4096]{1,0:T(8,128)(2,1)S(1)} %shard_map.68._.refs_0_, ...), custom_call_target="tpu_custom_call" | custom-call | bytes 33554432 | tf_op jit(solution)/shard_map/pallas_call | solution.py:27
  19.2 2.0 %collective-permute-start.4 = (f32[8,2048]{1,0:T(8,128)S(1)}, f32[8,2048]{1,0:T(8,128)S(1)}, u32[]{:S(2)}, u32[]{:S(2)}) collective-permute-start(f32[8,2048]{1,0:T(8,128)S(1)} %get-tuple-element.25), channel_id=1, source_target_pairs={{0,1},{1,0},{2,3},{3,2},{4,5},{5,4},{6,7},{7,6},{8,9},{9,8},{10,11... | collective-permute-start | bytes 196616 | tf_op jit(solution)/shard_map/ppermute | solution.py:207
  21.3 2.6 %collective-permute-start.5 = (f32[8,2048]{1,0:T(8,128)S(1)}, f32[8,2048]{1,0:T(8,128)S(1)}, u32[]{:S(2)}, u32[]{:S(2)}) collective-permute-start(f32[8,2048]{1,0:T(8,128)S(1)} %get-tuple-element.26), channel_id=1, source_target_pairs={{0,2},{1,3},{2,0},{3,1},{4,6},{5,7},{6,4},{7,5},{8,10},{9,11},{10,... | collective-permute-start | bytes 196616 | tf_op jit(solution)/shard_map/ppermute | solution.py:207
  23.9 2.7 %shard_map.71 = (bf16[2048,1280]{1,0:T(8,128)(2,1)S(1)}, bf16[2048,1280]{1,0:T(8,128)(2,1)S(1)}) custom-call(f32[1280,2048]{1,0:T(8,128)S(1)} %shard_map.69.refs_4_.b_ref, f32[1280,2048]{1,0:T(8,128)S(1)} %get-tuple-element.28.refs_0_.refs_6_.b_ref, f32[768,2048]{1,0:T(8,128)S(1)} %get-tuple-element.29.refs_1_.refs_7_.refs_0_.refs_8_, ...), custom_call_target="tpu_custom_call" | custom-call | bytes 16777216 | tf_op jit(solution)/shard_map/pallas_call | solution.py:27
  26.6 1.4 %collective-permute-done.5.refs_2_ = f32[8,2048]{1,0:T(8,128)S(1)} collective-permute-done((f32[8,2048]{1,0:T(8,128)S(1)}, f32[8,2048]{1,0:T(8,128)S(1)}, u32[]{:S(2)}, u32[]{:S(2)}) %collective-permute-start.5) | collective-permute-done | bytes 65568 | tf_op jit(solution)/shard_map/ppermute | solution.py:207
  28.0 1.9 %collective-permute-done.6.refs_3_ = f32[8,2048]{1,0:T(8,128)S(1)} collective-permute-done((f32[8,2048]{1,0:T(8,128)S(1)}, f32[8,2048]{1,0:T(8,128)S(1)}, u32[]{:S(2)}, u32[]{:S(2)}) %collective-permute-start.6) | collective-permute-done | bytes 65568 | tf_op jit(solution)/shard_map/ppermute | solution.py:207
  29.9 0.1 shard_map.72
  30.0 1.3 %collective-permute-start.9 = (f32[8,2048]{1,0:T(8,128)S(1)}, f32[8,2048]{1,0:T(8,128)S(1)}, u32[]{:S(2)}, u32[]{:S(2)}) collective-permute-start(f32[8,2048]{1,0:T(8,128)S(1)} %get-tuple-element.33.refs_0_), channel_id=1, source_target_pairs={{0,3},{1,2},{2,1},{3,0},{4,7},{5,6},{6,5},{7,4},{8,11},{9,10},{10,... | collective-permute-start | bytes 196616 | tf_op jit(solution)/shard_map/ppermute | solution.py:207
  31.3 3.1 %collective-permute-start.7 = (f32[8,2048]{1,0:T(8,128)S(1)}, f32[8,2048]{1,0:T(8,128)S(1)}, u32[]{:S(2)}, u32[]{:S(2)}) collective-permute-start(f32[8,2048]{1,0:T(8,128)S(1)} %get-tuple-element.33.refs_0_), channel_id=1, source_target_pairs={{0,1},{1,0},{2,3},{3,2},{4,5},{5,4},{6,7},{7,6},{8,9},{9,8},{10,11... | collective-permute-start | bytes 196616 | tf_op jit(solution)/shard_map/ppermute | solution.py:207
  34.4 2.7 %shard_map.73 = (bf16[2048,1280]{1,0:T(8,128)(2,1)S(1)}, bf16[2048,1280]{1,0:T(8,128)(2,1)S(1)}) custom-call(f32[1280,2048]{1,0:T(8,128)S(1)} %get-tuple-element.28.refs_0_.refs_6_.b_ref, f32[768,2048]{1,0:T(8,128)S(1)} %get-tuple-element.29.refs_1_.refs_7_.refs_0_.refs_8_, f32[768,2048]{1,0:T(8,128)S(1)} %get-tuple-element.30.refs_2_.refs_8_.refs_1_.refs_9_), custom_call_target="tpu_custom_call" | custom-call | bytes 16777216 | tf_op jit(solution)/shard_map/pallas_call | solution.py:27
  37.2 0.3 collective-permute-done.8.refs_2_
  37.5 6.1 %shard_map.74 = (f32[4,4,4096]{2,1,0:T(4,128)S(1)}, f32[4,4,4096]{2,1,0:T(4,128)S(1)}) custom-call(f32[8,2048]{1,0:T(8,128)S(1)} %get-tuple-element.33.refs_0_, f32[8,2048]{1,0:T(8,128)S(1)} %collective-permute-done.7.refs_1_, f32[8,2048]{1,0:T(8,128)S(1)} %collective-permute-done.8.refs_2_, f32[8,2048]{1,0:T(8,128)S(1)} %collective-permute-done.9.refs_3_, ...), custom_call_target="tpu_custom_call" | custom-call | bytes 33554432 | tf_op jit(solution)/shard_map/pallas_call | solution.py:27
  43.7 0.1 collective-permute-start.10
  43.7 1.5 %collective-permute-done.10.got = f32[4,4,4096]{2,1,0:T(4,128)S(1)} collective-permute-done((f32[4,4,4096]{2,1,0:T(4,128)S(1)}, f32[4,4,4096]{2,1,0:T(4,128)S(1)}, u32[]{:S(2)}, u32[]{:S(2)}) %collective-permute-start.10) | collective-permute-done | bytes 262176 | tf_op jit(solution)/shard_map/ppermute | solution.py:207
  45.3 0.1 shard_map.75
  45.3 1.6 %collective-permute-start.11 = (f32[4,4096]{1,0:T(4,128)S(1)}, f32[4,4096]{1,0:T(4,128)S(1)}, u32[]{:S(2)}, u32[]{:S(2)}) collective-permute-start(f32[4,4096]{1,0:T(4,128)S(1)} %get-tuple-element.39), channel_id=1, source_target_pairs={{0,8},{4,12},{8,0},{12,4},{16,24},{20,28},{24,16},{28,20},{1,9},{5... | collective-permute-start | bytes 196616 | tf_op jit(solution)/shard_map/ppermute | solution.py:207
  46.9 1.5 %collective-permute-start.12 = (f32[4,4096]{1,0:T(4,128)S(1)}, f32[4,4096]{1,0:T(4,128)S(1)}, u32[]{:S(2)}, u32[]{:S(2)}) collective-permute-start(f32[4,4096]{1,0:T(4,128)S(1)} %get-tuple-element.40), channel_id=1, source_target_pairs={{0,16},{4,20},{8,24},{12,28},{16,0},{20,4},{24,8},{28,12},{1,17},{... | collective-permute-start | bytes 196616 | tf_op jit(solution)/shard_map/ppermute | solution.py:207
  48.4 0.5 collective-permute-start.13
  48.9 0.7 %shard_map.76 = (f32[8,2048]{1,0:T(8,128)}, f32[8,2048]{1,0:T(8,128)}) custom-call(f32[8,2048]{1,0:T(8,128)S(1)} %copy-done, f32[8,2048]{1,0:T(8,128)S(1)} %copy-done.1, f32[8,2048]{1,0:T(8,128)S(1)} %get-tuple-element.42.rotated), custom_call_target="tpu_custom_call" | custom-call | bytes 524288 | tf_op jit(solution)/shard_map/pallas_call | solution.py:27
  49.5 0.1 collective-permute-done.11
  49.6 1.5 %collective-permute-done.12 = f32[4,4096]{1,0:T(4,128)S(1)} collective-permute-done((f32[4,4096]{1,0:T(4,128)S(1)}, f32[4,4096]{1,0:T(4,128)S(1)}, u32[]{:S(2)}, u32[]{:S(2)}) %collective-permute-start.12) | collective-permute-done | bytes 65568 | tf_op jit(solution)/shard_map/ppermute | solution.py:207
  51.1 2.4 %collective-permute-done.13 = f32[4,4096]{1,0:T(4,128)S(1)} collective-permute-done((f32[4,4096]{1,0:T(4,128)S(1)}, f32[4,4096]{1,0:T(4,128)S(1)}, u32[]{:S(2)}, u32[]{:S(2)}) %collective-permute-start.13) | collective-permute-done | bytes 65568 | tf_op jit(solution)/shard_map/ppermute | solution.py:207
  53.5 0.7 %add_add_fusion = f32[4,4096]{1,0:T(4,128)} fusion(f32[4,4096]{1,0:T(4,128)S(1)} %collective-permute-done.13, f32[4,4096]{1,0:T(4,128)S(1)} %collective-permute-done.12, f32[4,4096]{1,0:T(4,128)S(1)} %get-tuple-element.38, f32[4,4096]{1,0:T(4,128)S(1)} %collective-permute-done.11), kind=kLoop, calls=%fused_computation | loop fusion | flops 49152 | bytes 327680 | tf_op jit(solution)/shard_map/add | solution.py:284
  (11 shorter events, 0.0 us)
Async XLA Ops:
  0.6 1.6 %collective-permute-start = (bf16[4,4096]{1,0:T(4,128)(2,1)}, bf16[4,4096]{1,0:T(4,128)(2,1)S(1)}, u32[]{:S(2)}, u32[]{:S(2)}) collective-permute-start(bf16[4,4096]{1,0:T(4,128)(2,1)} %far.1), channel_id=1, source_target_pairs={{0,4},{4,0},{8,12},{12,8},{16,20},{20,16},{24,28},{28,24},{1,5},{5... | collective-permute-start | bytes 98312 | tf_op jit(solution)/shard_map/ppermute | solution.py:207
  2.3 8.6 %collective-permute-start.3 = (bf16[8,4096]{1,0:T(8,128)(2,1)S(1)}, bf16[8,4096]{1,0:T(8,128)(2,1)S(1)}, u32[]{:S(2)}, u32[]{:S(2)}) collective-permute-start(bf16[8,4096]{1,0:T(8,128)(2,1)S(1)} %shard_map.68._.refs_0_), channel_id=1, source_target_pairs={{0,24},{4,28},{8,16},{12,20},{16,8},{20,12},{24,0},{28,4},{1,25},{... | collective-permute-start | bytes 196616 | tf_op jit(solution)/shard_map/ppermute | solution.py:207
  6.1 4.8 %collective-permute-start.2 = (bf16[8,4096]{1,0:T(8,128)(2,1)S(1)}, bf16[8,4096]{1,0:T(8,128)(2,1)S(1)}, u32[]{:S(2)}, u32[]{:S(2)}) collective-permute-start(bf16[8,4096]{1,0:T(8,128)(2,1)S(1)} %shard_map.68._.refs_0_), channel_id=1, source_target_pairs={{0,16},{4,20},{8,24},{12,28},{16,0},{20,4},{24,8},{28,12},{1,17},{... | collective-permute-start | bytes 196616 | tf_op jit(solution)/shard_map/ppermute | solution.py:207
  6.6 4.3 %collective-permute-start.1 = (bf16[8,4096]{1,0:T(8,128)(2,1)S(1)}, bf16[8,4096]{1,0:T(8,128)(2,1)S(1)}, u32[]{:S(2)}, u32[]{:S(2)}) collective-permute-start(bf16[8,4096]{1,0:T(8,128)(2,1)S(1)} %shard_map.68._.refs_0_), channel_id=1, source_target_pairs={{0,8},{4,12},{8,0},{12,4},{16,24},{20,28},{24,16},{28,20},{1,9},{5... | collective-permute-start | bytes 196616 | tf_op jit(solution)/shard_map/ppermute | solution.py:207
  19.2 7.4 %collective-permute-start.4 = (f32[8,2048]{1,0:T(8,128)S(1)}, f32[8,2048]{1,0:T(8,128)S(1)}, u32[]{:S(2)}, u32[]{:S(2)}) collective-permute-start(f32[8,2048]{1,0:T(8,128)S(1)} %get-tuple-element.25), channel_id=1, source_target_pairs={{0,1},{1,0},{2,3},{3,2},{4,5},{5,4},{6,7},{7,6},{8,9},{9,8},{10,11... | collective-permute-start | bytes 196616 | tf_op jit(solution)/shard_map/ppermute | solution.py:207
  21.3 6.7 %collective-permute-start.5 = (f32[8,2048]{1,0:T(8,128)S(1)}, f32[8,2048]{1,0:T(8,128)S(1)}, u32[]{:S(2)}, u32[]{:S(2)}) collective-permute-start(f32[8,2048]{1,0:T(8,128)S(1)} %get-tuple-element.26), channel_id=1, source_target_pairs={{0,2},{1,3},{2,0},{3,1},{4,6},{5,7},{6,4},{7,5},{8,10},{9,11},{10,... | collective-permute-start | bytes 196616 | tf_op jit(solution)/shard_map/ppermute | solution.py:207
  23.9 6.1 %collective-permute-start.6 = (f32[8,2048]{1,0:T(8,128)S(1)}, f32[8,2048]{1,0:T(8,128)S(1)}, u32[]{:S(2)}, u32[]{:S(2)}) collective-permute-start(f32[8,2048]{1,0:T(8,128)S(1)} %get-tuple-element.27), channel_id=1, source_target_pairs={{0,3},{1,2},{2,1},{3,0},{4,7},{5,6},{6,5},{7,4},{8,11},{9,10},{10,... | collective-permute-start | bytes 196616 | tf_op jit(solution)/shard_map/ppermute | solution.py:207
  23.9 6.1 %copy-start = (f32[8,2048]{1,0:T(8,128)S(1)}, f32[8,2048]{1,0:T(8,128)}, u32[]{:S(2)}) copy-start(f32[8,2048]{1,0:T(8,128)} %m_ref.3) | copy-start | bytes 196612
  23.9 6.1 %copy-start.1 = (f32[8,2048]{1,0:T(8,128)S(1)}, f32[8,2048]{1,0:T(8,128)}, u32[]{:S(2)}) copy-start(f32[8,2048]{1,0:T(8,128)} %s_ref.3) | copy-start | bytes 196612
  30.0 7.2 %collective-permute-start.9 = (f32[8,2048]{1,0:T(8,128)S(1)}, f32[8,2048]{1,0:T(8,128)S(1)}, u32[]{:S(2)}, u32[]{:S(2)}) collective-permute-start(f32[8,2048]{1,0:T(8,128)S(1)} %get-tuple-element.33.refs_0_), channel_id=1, source_target_pairs={{0,3},{1,2},{2,1},{3,0},{4,7},{5,6},{6,5},{7,4},{8,11},{9,10},{10,... | collective-permute-start | bytes 196616 | tf_op jit(solution)/shard_map/ppermute | solution.py:207
  31.3 6.2 %collective-permute-start.8 = (f32[8,2048]{1,0:T(8,128)S(1)}, f32[8,2048]{1,0:T(8,128)S(1)}, u32[]{:S(2)}, u32[]{:S(2)}) collective-permute-start(f32[8,2048]{1,0:T(8,128)S(1)} %get-tuple-element.33.refs_0_), channel_id=1, source_target_pairs={{0,2},{1,3},{2,0},{3,1},{4,6},{5,7},{6,4},{7,5},{8,10},{9,11},{10,... | collective-permute-start | bytes 196616 | tf_op jit(solution)/shard_map/ppermute | solution.py:207
  31.3 6.2 %collective-permute-start.7 = (f32[8,2048]{1,0:T(8,128)S(1)}, f32[8,2048]{1,0:T(8,128)S(1)}, u32[]{:S(2)}, u32[]{:S(2)}) collective-permute-start(f32[8,2048]{1,0:T(8,128)S(1)} %get-tuple-element.33.refs_0_), channel_id=1, source_target_pairs={{0,1},{1,0},{2,3},{3,2},{4,5},{5,4},{6,7},{7,6},{8,9},{9,8},{10,11... | collective-permute-start | bytes 196616 | tf_op jit(solution)/shard_map/ppermute | solution.py:207
  43.7 1.6 %collective-permute-start.10 = (f32[4,4,4096]{2,1,0:T(4,128)S(1)}, f32[4,4,4096]{2,1,0:T(4,128)S(1)}, u32[]{:S(2)}, u32[]{:S(2)}) collective-permute-start(f32[4,4,4096]{2,1,0:T(4,128)S(1)} %get-tuple-element.37), channel_id=1, source_target_pairs={{0,4},{4,0},{8,12},{12,8},{16,20},{20,16},{24,28},{28,24},{1,5},{5... | collective-permute-start | bytes 786440 | tf_op jit(solution)/shard_map/ppermute | solution.py:207
  45.3 4.3 %collective-permute-start.11 = (f32[4,4096]{1,0:T(4,128)S(1)}, f32[4,4096]{1,0:T(4,128)S(1)}, u32[]{:S(2)}, u32[]{:S(2)}) collective-permute-start(f32[4,4096]{1,0:T(4,128)S(1)} %get-tuple-element.39), channel_id=1, source_target_pairs={{0,8},{4,12},{8,0},{12,4},{16,24},{20,28},{24,16},{28,20},{1,9},{5... | collective-permute-start | bytes 196616 | tf_op jit(solution)/shard_map/ppermute | solution.py:207
  46.9 4.3 %collective-permute-start.12 = (f32[4,4096]{1,0:T(4,128)S(1)}, f32[4,4096]{1,0:T(4,128)S(1)}, u32[]{:S(2)}, u32[]{:S(2)}) collective-permute-start(f32[4,4096]{1,0:T(4,128)S(1)} %get-tuple-element.40), channel_id=1, source_target_pairs={{0,16},{4,20},{8,24},{12,28},{16,0},{20,4},{24,8},{28,12},{1,17},{... | collective-permute-start | bytes 196616 | tf_op jit(solution)/shard_map/ppermute | solution.py:207
  48.4 5.2 %collective-permute-start.13 = (f32[4,4096]{1,0:T(4,128)S(1)}, f32[4,4096]{1,0:T(4,128)S(1)}, u32[]{:S(2)}, u32[]{:S(2)}) collective-permute-start(f32[4,4096]{1,0:T(4,128)S(1)} %get-tuple-element.41), channel_id=1, source_target_pairs={{0,24},{4,28},{8,16},{12,20},{16,8},{20,12},{24,0},{28,4},{1,25},{... | collective-permute-start | bytes 196616 | tf_op jit(solution)/shard_map/ppermute | solution.py:207

commit v6 on v5

--- a/solution.py
+++ b/solution.py
@@ -103,9 +103,19 @@
         k = begins[p] + i
         return pltpu.make_async_copy(b_ref.at[span(k, rows), :], parts[p - 1].at[span(i, rows), :], sems.at[k])
 
+    end = len(PARTS) - 1
+    half = rows // 2
+
+    def half_copy(h):
+        far = pl.ds(b_ref.shape[0] - rows + h * half, half)
+        near = pl.ds((PARTS[end] - 1) * rows + h * half, half)
+        return pltpu.make_async_copy(b_ref.at[far, :], parts[end - 1].at[near, :], sems.at[15 + h])
+
     for p in range(1, len(PARTS)):
-        for i in range(PARTS[p]):
+        for i in range(PARTS[p] - (p == end)):
             copy(p, i).start()
+    for h in range(2):
+        half_copy(h).start()
     g_ref[...] = jnp.concatenate([block[...].astype(F32) for block in blocks], axis=0).astype(BF16)
     total[...] = jnp.zeros_like(total)
     for p, ref in enumerate((ready, *parts)):
@@ -122,7 +132,16 @@
                 )
             return 0
 
-        lax.fori_loop(0, PARTS[p], tile, 0)
+        lax.fori_loop(0, PARTS[p] - (p == end), tile, 0)
+    for h in range(2):
+        half_copy(h).wait()
+        begin = b_ref.shape[0] - rows + h * half
+        near = (PARTS[end] - 1) * rows + h * half
+        for j in range(width // columns):
+            at = slice(j * columns, (j + 1) * columns)
+            high, low = split(parts[end - 1][near : near + half, at])
+            g = g_ref[:, begin : begin + half]
+            total[:, at] += jnp.dot(g, high, preferred_element_type=F32) + jnp.dot(g, low, preferred_element_type=F32)
     pair = blocks[0].shape[0]
     chip = lax.axis_index("rows") // 2
     each = chips // n
@@ -240,7 +259,7 @@
         [
             pltpu.VMEM((n * each, height), BF16),
             pltpu.VMEM((n * each, width), F32),
-            pltpu.SemaphoreType.DMA((16,)),
+            pltpu.SemaphoreType.DMA((17,)),
         ],
         moved,
     )

time: 54.4 us -> 54.3 us (level)
  no operation moved by 1% of the time
where the time goes in v6:
time: 54.3 us; the launch traced here: 54.1 us
  Pallas kernels  25.5 us (47%)
  starting transfers between devices  17.8 us (33%)
  waiting for transfers between devices  9.45 us (17%)
  between operations  0.74 us (1%)
  other arithmetic  0.67 us (1%)
    pallas_call x10, Pallas kernels, kernel(): pl.pallas_call(body, out_shape=outs, in_specs=ins, out_specs=jax.tree.map...  25.5 us
    ppermute x14, starting transfers between devices, along(): return lax.ppermute(x, axis, [(i, i ^ s) for i in range(size)])  17.8 us
    ppermute x14, waiting for transfers between devices, along(): return lax.ppermute(x, axis, [(i, i ^ s) for i in range(size)])  9.45 us
  transfers between devices with their start and end apart: 14, of which 8 were waited for; matrix products, arithmetic and copies ran while one was open for 0% of the time, Pallas kernels for 20%

profile of v6, /device:TPU:0, one launch (start us, length us, event | category | flops | bytes accessed | tf_op | source)
XLA Modules:
  0.0 54.1 jit_solution(8828739488926527068)
XLA Ops:
  0.6 0.6 %collective-permute-start = (bf16[4,4096]{1,0:T(4,128)(2,1)}, bf16[4,4096]{1,0:T(4,128)(2,1)S(1)}, u32[]{:S(2)}, u32[]{:S(2)}) collective-permute-start(bf16[4,4096]{1,0:T(4,128)(2,1)} %far.1), channel_id=1, source_target_pairs={{0,4},{4,0},{8,12},{12,8},{16,20},{20,16},{24,28},{28,24},{1,5},{5... | collective-permute-start | bytes 98312 | tf_op jit(solution)/shard_map/ppermute | solution.py:226
  1.2 0.8 %shard_map.67.own = bf16[4,4096]{1,0:T(4,128)(2,1)S(1)} custom-call(bf16[4,4096]{1,0:T(4,128)(2,1)} %far.1), custom_call_target="tpu_custom_call" | custom-call | bytes 65536 | tf_op jit(solution)/shard_map/pallas_call | solution.py:27
  2.0 0.3 collective-permute-done.got
  2.3 3.8 %collective-permute-start.3 = (bf16[8,4096]{1,0:T(8,128)(2,1)S(1)}, bf16[8,4096]{1,0:T(8,128)(2,1)S(1)}, u32[]{:S(2)}, u32[]{:S(2)}) collective-permute-start(bf16[8,4096]{1,0:T(8,128)(2,1)S(1)} %shard_map.68._.refs_0_), channel_id=1, source_target_pairs={{0,24},{4,28},{8,16},{12,20},{16,8},{20,12},{24,0},{28,4},{1,25},{... | collective-permute-start | bytes 196616 | tf_op jit(solution)/shard_map/ppermute | solution.py:226
  6.1 0.5 collective-permute-start.2
  6.6 0.1 collective-permute-start.1
  6.8 4.1 %shard_map.69.refs_4_.b_ref = f32[1280,2048]{1,0:T(8,128)S(1)} custom-call(bf16[8,4096]{1,0:T(8,128)(2,1)S(1)} %shard_map.68._.refs_0_, f32[4096,2048]{1,0:T(8,128)} %refs_5_.1), custom_call_target="tpu_custom_call" | custom-call | bytes 16777216 | tf_op jit(solution)/shard_map/pallas_call | solution.py:27
  10.9 0.0 collective-permute-done.3.refs_3_
  10.9 0.0 collective-permute-done.1.refs_1_
  10.9 8.2 %shard_map.70 = (f32[8,2048]{1,0:T(8,128)S(1)}, f32[8,2048]{1,0:T(8,128)S(1)}, f32[8,2048]{1,0:T(8,128)S(1)}, f32[8,2048]{1,0:T(8,128)S(1)}, f32[1280,2048]{1,0:...) custom-call(bf16[8,4096]{1,0:T(8,128)(2,1)S(1)} %shard_map.68._.refs_0_, ...), custom_call_target="tpu_custom_call" | custom-call | bytes 33554432 | tf_op jit(solution)/shard_map/pallas_call | solution.py:27
  19.1 2.0 %collective-permute-start.4 = (f32[8,2048]{1,0:T(8,128)S(1)}, f32[8,2048]{1,0:T(8,128)S(1)}, u32[]{:S(2)}, u32[]{:S(2)}) collective-permute-start(f32[8,2048]{1,0:T(8,128)S(1)} %get-tuple-element.25), channel_id=1, source_target_pairs={{0,1},{1,0},{2,3},{3,2},{4,5},{5,4},{6,7},{7,6},{8,9},{9,8},{10,11... | collective-permute-start | bytes 196616 | tf_op jit(solution)/shard_map/ppermute | solution.py:226
  21.1 2.6 %collective-permute-start.5 = (f32[8,2048]{1,0:T(8,128)S(1)}, f32[8,2048]{1,0:T(8,128)S(1)}, u32[]{:S(2)}, u32[]{:S(2)}) collective-permute-start(f32[8,2048]{1,0:T(8,128)S(1)} %get-tuple-element.26), channel_id=1, source_target_pairs={{0,2},{1,3},{2,0},{3,1},{4,6},{5,7},{6,4},{7,5},{8,10},{9,11},{10,... | collective-permute-start | bytes 196616 | tf_op jit(solution)/shard_map/ppermute | solution.py:226
  23.7 2.7 %shard_map.71 = (bf16[2048,1280]{1,0:T(8,128)(2,1)S(1)}, bf16[2048,1280]{1,0:T(8,128)(2,1)S(1)}) custom-call(f32[1280,2048]{1,0:T(8,128)S(1)} %shard_map.69.refs_4_.b_ref, f32[1280,2048]{1,0:T(8,128)S(1)} %get-tuple-element.28.refs_0_.refs_6_.b_ref, f32[768,2048]{1,0:T(8,128)S(1)} %get-tuple-element.29.refs_1_.refs_7_.refs_0_.refs_8_, ...), custom_call_target="tpu_custom_call" | custom-call | bytes 16777216 | tf_op jit(solution)/shard_map/pallas_call | solution.py:27
  26.5 1.4 %collective-permute-done.5.refs_2_ = f32[8,2048]{1,0:T(8,128)S(1)} collective-permute-done((f32[8,2048]{1,0:T(8,128)S(1)}, f32[8,2048]{1,0:T(8,128)S(1)}, u32[]{:S(2)}, u32[]{:S(2)}) %collective-permute-start.5) | collective-permute-done | bytes 65568 | tf_op jit(solution)/shard_map/ppermute | solution.py:226
  27.9 1.9 %collective-permute-done.6.refs_3_ = f32[8,2048]{1,0:T(8,128)S(1)} collective-permute-done((f32[8,2048]{1,0:T(8,128)S(1)}, f32[8,2048]{1,0:T(8,128)S(1)}, u32[]{:S(2)}, u32[]{:S(2)}) %collective-permute-start.6) | collective-permute-done | bytes 65568 | tf_op jit(solution)/shard_map/ppermute | solution.py:226
  29.8 0.1 shard_map.72
  29.9 1.3 %collective-permute-start.9 = (f32[8,2048]{1,0:T(8,128)S(1)}, f32[8,2048]{1,0:T(8,128)S(1)}, u32[]{:S(2)}, u32[]{:S(2)}) collective-permute-start(f32[8,2048]{1,0:T(8,128)S(1)} %get-tuple-element.33.refs_0_), channel_id=1, source_target_pairs={{0,3},{1,2},{2,1},{3,0},{4,7},{5,6},{6,5},{7,4},{8,11},{9,10},{10,... | collective-permute-start | bytes 196616 | tf_op jit(solution)/shard_map/ppermute | solution.py:226
  31.2 3.1 %collective-permute-start.7 = (f32[8,2048]{1,0:T(8,128)S(1)}, f32[8,2048]{1,0:T(8,128)S(1)}, u32[]{:S(2)}, u32[]{:S(2)}) collective-permute-start(f32[8,2048]{1,0:T(8,128)S(1)} %get-tuple-element.33.refs_0_), channel_id=1, source_target_pairs={{0,1},{1,0},{2,3},{3,2},{4,5},{5,4},{6,7},{7,6},{8,9},{9,8},{10,11... | collective-permute-start | bytes 196616 | tf_op jit(solution)/shard_map/ppermute | solution.py:226
  34.3 2.7 %shard_map.73 = (bf16[2048,1280]{1,0:T(8,128)(2,1)S(1)}, bf16[2048,1280]{1,0:T(8,128)(2,1)S(1)}) custom-call(f32[1280,2048]{1,0:T(8,128)S(1)} %get-tuple-element.28.refs_0_.refs_6_.b_ref, f32[768,2048]{1,0:T(8,128)S(1)} %get-tuple-element.29.refs_1_.refs_7_.refs_0_.refs_8_, f32[768,2048]{1,0:T(8,128)S(1)} %get-tuple-element.30.refs_2_.refs_8_.refs_1_.refs_9_), custom_call_target="tpu_custom_call" | custom-call | bytes 16777216 | tf_op jit(solution)/shard_map/pallas_call | solution.py:27
  37.1 0.3 collective-permute-done.8.refs_2_
  37.4 6.1 %shard_map.74 = (f32[4,4,4096]{2,1,0:T(4,128)S(1)}, f32[4,4,4096]{2,1,0:T(4,128)S(1)}) custom-call(f32[8,2048]{1,0:T(8,128)S(1)} %get-tuple-element.33.refs_0_, f32[8,2048]{1,0:T(8,128)S(1)} %collective-permute-done.7.refs_1_, f32[8,2048]{1,0:T(8,128)S(1)} %collective-permute-done.8.refs_2_, f32[8,2048]{1,0:T(8,128)S(1)} %collective-permute-done.9.refs_3_, ...), custom_call_target="tpu_custom_call" | custom-call | bytes 33554432 | tf_op jit(solution)/shard_map/pallas_call | solution.py:27
  43.5 0.1 collective-permute-start.10
  43.6 1.5 %collective-permute-done.10.got = f32[4,4,4096]{2,1,0:T(4,128)S(1)} collective-permute-done((f32[4,4,4096]{2,1,0:T(4,128)S(1)}, f32[4,4,4096]{2,1,0:T(4,128)S(1)}, u32[]{:S(2)}, u32[]{:S(2)}) %collective-permute-start.10) | collective-permute-done | bytes 262176 | tf_op jit(solution)/shard_map/ppermute | solution.py:226
  45.1 0.1 shard_map.75
  45.2 1.6 %collective-permute-start.11 = (f32[4,4096]{1,0:T(4,128)S(1)}, f32[4,4096]{1,0:T(4,128)S(1)}, u32[]{:S(2)}, u32[]{:S(2)}) collective-permute-start(f32[4,4096]{1,0:T(4,128)S(1)} %get-tuple-element.39), channel_id=1, source_target_pairs={{0,8},{4,12},{8,0},{12,4},{16,24},{20,28},{24,16},{28,20},{1,9},{5... | collective-permute-start | bytes 196616 | tf_op jit(solution)/shard_map/ppermute | solution.py:226
  46.7 1.5 %collective-permute-start.12 = (f32[4,4096]{1,0:T(4,128)S(1)}, f32[4,4096]{1,0:T(4,128)S(1)}, u32[]{:S(2)}, u32[]{:S(2)}) collective-permute-start(f32[4,4096]{1,0:T(4,128)S(1)} %get-tuple-element.40), channel_id=1, source_target_pairs={{0,16},{4,20},{8,24},{12,28},{16,0},{20,4},{24,8},{28,12},{1,17},{... | collective-permute-start | bytes 196616 | tf_op jit(solution)/shard_map/ppermute | solution.py:226
  48.3 0.5 collective-permute-start.13
  48.7 0.7 %shard_map.76 = (f32[8,2048]{1,0:T(8,128)}, f32[8,2048]{1,0:T(8,128)}) custom-call(f32[8,2048]{1,0:T(8,128)S(1)} %copy-done, f32[8,2048]{1,0:T(8,128)S(1)} %copy-done.1, f32[8,2048]{1,0:T(8,128)S(1)} %get-tuple-element.42.rotated), custom_call_target="tpu_custom_call" | custom-call | bytes 524288 | tf_op jit(solution)/shard_map/pallas_call | solution.py:27
  49.4 0.1 collective-permute-done.11
  49.5 1.5 %collective-permute-done.12 = f32[4,4096]{1,0:T(4,128)S(1)} collective-permute-done((f32[4,4096]{1,0:T(4,128)S(1)}, f32[4,4096]{1,0:T(4,128)S(1)}, u32[]{:S(2)}, u32[]{:S(2)}) %collective-permute-start.12) | collective-permute-done | bytes 65568 | tf_op jit(solution)/shard_map/ppermute | solution.py:226
  51.0 2.4 %collective-permute-done.13 = f32[4,4096]{1,0:T(4,128)S(1)} collective-permute-done((f32[4,4096]{1,0:T(4,128)S(1)}, f32[4,4096]{1,0:T(4,128)S(1)}, u32[]{:S(2)}, u32[]{:S(2)}) %collective-permute-start.13) | collective-permute-done | bytes 65568 | tf_op jit(solution)/shard_map/ppermute | solution.py:226
  53.4 0.7 %add_add_fusion = f32[4,4096]{1,0:T(4,128)} fusion(f32[4,4096]{1,0:T(4,128)S(1)} %collective-permute-done.13, f32[4,4096]{1,0:T(4,128)S(1)} %collective-permute-done.12, f32[4,4096]{1,0:T(4,128)S(1)} %get-tuple-element.38, f32[4,4096]{1,0:T(4,128)S(1)} %collective-permute-done.11), kind=kLoop, calls=%fused_computation | loop fusion | flops 49152 | bytes 327680 | tf_op jit(solution)/shard_map/add | solution.py:303
  (11 shorter events, 0.0 us)
Async XLA Ops:
  0.6 1.6 %collective-permute-start = (bf16[4,4096]{1,0:T(4,128)(2,1)}, bf16[4,4096]{1,0:T(4,128)(2,1)S(1)}, u32[]{:S(2)}, u32[]{:S(2)}) collective-permute-start(bf16[4,4096]{1,0:T(4,128)(2,1)} %far.1), channel_id=1, source_target_pairs={{0,4},{4,0},{8,12},{12,8},{16,20},{20,16},{24,28},{28,24},{1,5},{5... | collective-permute-start | bytes 98312 | tf_op jit(solution)/shard_map/ppermute | solution.py:226
  2.3 8.6 %collective-permute-start.3 = (bf16[8,4096]{1,0:T(8,128)(2,1)S(1)}, bf16[8,4096]{1,0:T(8,128)(2,1)S(1)}, u32[]{:S(2)}, u32[]{:S(2)}) collective-permute-start(bf16[8,4096]{1,0:T(8,128)(2,1)S(1)} %shard_map.68._.refs_0_), channel_id=1, source_target_pairs={{0,24},{4,28},{8,16},{12,20},{16,8},{20,12},{24,0},{28,4},{1,25},{... | collective-permute-start | bytes 196616 | tf_op jit(solution)/shard_map/ppermute | solution.py:226
  6.1 4.8 %collective-permute-start.2 = (bf16[8,4096]{1,0:T(8,128)(2,1)S(1)}, bf16[8,4096]{1,0:T(8,128)(2,1)S(1)}, u32[]{:S(2)}, u32[]{:S(2)}) collective-permute-start(bf16[8,4096]{1,0:T(8,128)(2,1)S(1)} %shard_map.68._.refs_0_), channel_id=1, source_target_pairs={{0,16},{4,20},{8,24},{12,28},{16,0},{20,4},{24,8},{28,12},{1,17},{... | collective-permute-start | bytes 196616 | tf_op jit(solution)/shard_map/ppermute | solution.py:226
  6.6 4.3 %collective-permute-start.1 = (bf16[8,4096]{1,0:T(8,128)(2,1)S(1)}, bf16[8,4096]{1,0:T(8,128)(2,1)S(1)}, u32[]{:S(2)}, u32[]{:S(2)}) collective-permute-start(bf16[8,4096]{1,0:T(8,128)(2,1)S(1)} %shard_map.68._.refs_0_), channel_id=1, source_target_pairs={{0,8},{4,12},{8,0},{12,4},{16,24},{20,28},{24,16},{28,20},{1,9},{5... | collective-permute-start | bytes 196616 | tf_op jit(solution)/shard_map/ppermute | solution.py:226
  19.1 7.4 %collective-permute-start.4 = (f32[8,2048]{1,0:T(8,128)S(1)}, f32[8,2048]{1,0:T(8,128)S(1)}, u32[]{:S(2)}, u32[]{:S(2)}) collective-permute-start(f32[8,2048]{1,0:T(8,128)S(1)} %get-tuple-element.25), channel_id=1, source_target_pairs={{0,1},{1,0},{2,3},{3,2},{4,5},{5,4},{6,7},{7,6},{8,9},{9,8},{10,11... | collective-permute-start | bytes 196616 | tf_op jit(solution)/shard_map/ppermute | solution.py:226
  21.1 6.7 %collective-permute-start.5 = (f32[8,2048]{1,0:T(8,128)S(1)}, f32[8,2048]{1,0:T(8,128)S(1)}, u32[]{:S(2)}, u32[]{:S(2)}) collective-permute-start(f32[8,2048]{1,0:T(8,128)S(1)} %get-tuple-element.26), channel_id=1, source_target_pairs={{0,2},{1,3},{2,0},{3,1},{4,6},{5,7},{6,4},{7,5},{8,10},{9,11},{10,... | collective-permute-start | bytes 196616 | tf_op jit(solution)/shard_map/ppermute | solution.py:226
  23.7 6.1 %collective-permute-start.6 = (f32[8,2048]{1,0:T(8,128)S(1)}, f32[8,2048]{1,0:T(8,128)S(1)}, u32[]{:S(2)}, u32[]{:S(2)}) collective-permute-start(f32[8,2048]{1,0:T(8,128)S(1)} %get-tuple-element.27), channel_id=1, source_target_pairs={{0,3},{1,2},{2,1},{3,0},{4,7},{5,6},{6,5},{7,4},{8,11},{9,10},{10,... | collective-permute-start | bytes 196616 | tf_op jit(solution)/shard_map/ppermute | solution.py:226
  23.7 6.1 %copy-start = (f32[8,2048]{1,0:T(8,128)S(1)}, f32[8,2048]{1,0:T(8,128)}, u32[]{:S(2)}) copy-start(f32[8,2048]{1,0:T(8,128)} %m_ref.3) | copy-start | bytes 196612
  23.7 6.1 %copy-start.1 = (f32[8,2048]{1,0:T(8,128)S(1)}, f32[8,2048]{1,0:T(8,128)}, u32[]{:S(2)}) copy-start(f32[8,2048]{1,0:T(8,128)} %s_ref.3) | copy-start | bytes 196612
  29.9 7.2 %collective-permute-start.9 = (f32[8,2048]{1,0:T(8,128)S(1)}, f32[8,2048]{1,0:T(8,128)S(1)}, u32[]{:S(2)}, u32[]{:S(2)}) collective-permute-start(f32[8,2048]{1,0:T(8,128)S(1)} %get-tuple-element.33.refs_0_), channel_id=1, source_target_pairs={{0,3},{1,2},{2,1},{3,0},{4,7},{5,6},{6,5},{7,4},{8,11},{9,10},{10,... | collective-permute-start | bytes 196616 | tf_op jit(solution)/shard_map/ppermute | solution.py:226
  31.2 6.2 %collective-permute-start.8 = (f32[8,2048]{1,0:T(8,128)S(1)}, f32[8,2048]{1,0:T(8,128)S(1)}, u32[]{:S(2)}, u32[]{:S(2)}) collective-permute-start(f32[8,2048]{1,0:T(8,128)S(1)} %get-tuple-element.33.refs_0_), channel_id=1, source_target_pairs={{0,2},{1,3},{2,0},{3,1},{4,6},{5,7},{6,4},{7,5},{8,10},{9,11},{10,... | collective-permute-start | bytes 196616 | tf_op jit(solution)/shard_map/ppermute | solution.py:226
  31.2 6.2 %collective-permute-start.7 = (f32[8,2048]{1,0:T(8,128)S(1)}, f32[8,2048]{1,0:T(8,128)S(1)}, u32[]{:S(2)}, u32[]{:S(2)}) collective-permute-start(f32[8,2048]{1,0:T(8,128)S(1)} %get-tuple-element.33.refs_0_), channel_id=1, source_target_pairs={{0,1},{1,0},{2,3},{3,2},{4,5},{5,4},{6,7},{7,6},{8,9},{9,8},{10,11... | collective-permute-start | bytes 196616 | tf_op jit(solution)/shard_map/ppermute | solution.py:226
  43.5 1.6 %collective-permute-start.10 = (f32[4,4,4096]{2,1,0:T(4,128)S(1)}, f32[4,4,4096]{2,1,0:T(4,128)S(1)}, u32[]{:S(2)}, u32[]{:S(2)}) collective-permute-start(f32[4,4,4096]{2,1,0:T(4,128)S(1)} %get-tuple-element.37), channel_id=1, source_target_pairs={{0,4},{4,0},{8,12},{12,8},{16,20},{20,16},{24,28},{28,24},{1,5},{5... | collective-permute-start | bytes 786440 | tf_op jit(solution)/shard_map/ppermute | solution.py:226
  45.2 4.3 %collective-permute-start.11 = (f32[4,4096]{1,0:T(4,128)S(1)}, f32[4,4096]{1,0:T(4,128)S(1)}, u32[]{:S(2)}, u32[]{:S(2)}) collective-permute-start(f32[4,4096]{1,0:T(4,128)S(1)} %get-tuple-element.39), channel_id=1, source_target_pairs={{0,8},{4,12},{8,0},{12,4},{16,24},{20,28},{24,16},{28,20},{1,9},{5... | collective-permute-start | bytes 196616 | tf_op jit(solution)/shard_map/ppermute | solution.py:226
  46.7 4.3 %collective-permute-start.12 = (f32[4,4096]{1,0:T(4,128)S(1)}, f32[4,4096]{1,0:T(4,128)S(1)}, u32[]{:S(2)}, u32[]{:S(2)}) collective-permute-start(f32[4,4096]{1,0:T(4,128)S(1)} %get-tuple-element.40), channel_id=1, source_target_pairs={{0,16},{4,20},{8,24},{12,28},{16,0},{20,4},{24,8},{28,12},{1,17},{... | collective-permute-start | bytes 196616 | tf_op jit(solution)/shard_map/ppermute | solution.py:226
  48.3 5.2 %collective-permute-start.13 = (f32[4,4096]{1,0:T(4,128)S(1)}, f32[4,4096]{1,0:T(4,128)S(1)}, u32[]{:S(2)}, u32[]{:S(2)}) collective-permute-start(f32[4,4096]{1,0:T(4,128)S(1)} %get-tuple-element.41), channel_id=1, source_target_pairs={{0,24},{4,28},{8,16},{12,20},{16,8},{20,12},{24,0},{28,4},{1,25},{... | collective-permute-start | bytes 196616 | tf_op jit(solution)/shard_map/ppermute | solution.py:226
